TPU v7x, 32 devices: a whole 2x2x4 slice. The times are simulated.
32 devices in a mesh: sub: 16 (over z, y, core), strip: 2 (over x).
Axes of the slice: x: 2, y: 2, z: 4, core: 2. Of those that a mesh axis runs over, the one named last changes fastest.
Arguments:
- spectra: bfloat16 [32, 256, 2048], P('sub', 'strip'), may hold values from -6 to 6
- offsets: int32 [32], P('sub'), may hold values from 0 to 1023
Outputs:
- foreground: float32 [1024, 256, 32], P('strip', 'sub')
All inputs are finite; a program needn't handle non-finite values.
Results may differ from a plain program's by a relative error of at most 0.0068.
Values may be sent and summed in bfloat16 or wider, within the bound.
A program may use at most 64 MiB of HBM per device.

v0:
```python
import math

import jax
import jax.numpy as jnp
import numpy as np
from jax import lax
from jax.sharding import PartitionSpec as P

KR = 256
ROWS = 1024
COLS = 256
WIN = 8
BG = 16


def from_behind(value, axis, steps):
    count = lax.axis_size(axis)
    pairs = [(source, (source + steps) % count) for source in range(count)]
    return lax.ppermute(value, axis, pairs)


def extended(shard, sides, width):
    for axis, dim in sides:
        count, length = (lax.axis_size(axis), shard.shape[dim])
        up = [(i, (i + 1) % count) for i in range(count - 1)]
        down = [(j, i) for i, j in up]
        last = lax.slice_in_dim(shard, length - width, length, axis=dim)
        leading = lax.slice_in_dim(shard, 0, width, axis=dim)
        before = lax.ppermute(last, axis, up)
        after = lax.ppermute(leading, axis, down)
        shard = jnp.concatenate([before, shard, after], axis=dim)
    return shard


def column_table(samples, width):
    sample_index = jnp.arange(samples, dtype=jnp.int32)[:, None]
    column_index = jnp.arange(width, dtype=jnp.int32)[None, :]
    phase = jnp.mod(sample_index * column_index, samples).astype(jnp.float32) * (
        2.0 * math.pi / samples
    )
    cosine = jnp.cos(phase) / math.sqrt(samples)
    sine = -jnp.sin(phase) / math.sqrt(samples)
    upper = jnp.concatenate([cosine, sine], axis=1)
    lower = jnp.concatenate([-sine, cosine], axis=1)
    return jnp.concatenate([upper, lower], axis=0).astype(jnp.bfloat16)


def row_table(row_index, samples, image_rows):
    sample_index = jnp.arange(samples, dtype=jnp.int32)[None, :] - samples // 2
    phase = jnp.mod(row_index[:, None] * sample_index, image_rows).astype(jnp.float32) * (
        2.0 * math.pi / image_rows
    )
    scale = 1.0 / math.sqrt(samples)
    return jnp.concatenate([jnp.cos(phase) * scale, jnp.sin(phase) * scale], axis=0).astype(
        jnp.bfloat16
    )


def apply_phase(mixed, offsets, sample_index):
    angle = jnp.mod(offsets[:, None] * (sample_index[None, :] - KR // 2), ROWS).astype(
        jnp.float32
    ) * (2.0 * math.pi / ROWS)
    cosine = jnp.cos(angle)[:, :, None]
    sine = jnp.sin(angle)[:, :, None]
    real_part = mixed[:, :, :COLS]
    imag_part = mixed[:, :, COLS:]
    return jnp.concatenate(
        [real_part * cosine - imag_part * sine, real_part * sine + imag_part * cosine], axis=2
    ).astype(jnp.bfloat16)


def window_mask(block_offset, count):
    target = np.arange(count)[:, None]
    source = np.arange(count)[None, :]
    distance = block_offset * count + source - target
    return ((distance >= 0) & (distance < WIN)).astype(np.float32)


def combine_parts(product, strip_rows):
    product = lax.optimization_barrier(product)
    real_part = product[:, :strip_rows, :COLS] - product[:, strip_rows:, COLS:]
    imag_part = product[:, :strip_rows, COLS:] + product[:, strip_rows:, :COLS]
    return jnp.concatenate([real_part, imag_part], axis=2)


def remove_background(stack):
    frame_count = stack.shape[0]
    series = jnp.transpose(stack, (1, 2, 0))
    source = jnp.arange(frame_count, dtype=jnp.int32)[:, None]
    target = jnp.arange(frame_count, dtype=jnp.int32)[None, :]
    behind = jnp.where(jnp.mod(target - source, frame_count) < BG, 1.0 / BG, 0.0).astype(
        jnp.float32
    )
    weights = jnp.where(source == target, 1.0, 0.0).astype(jnp.float32) - behind
    return jnp.einsum("rcg,gf->rcf", series, weights, precision=lax.Precision.HIGHEST)


def body(spectra, offsets):
    sub_dev = spectra.shape[0]
    strip_rows = ROWS // lax.axis_size("strip")
    local_samples = spectra.shape[1]
    first_row = lax.axis_index("strip") * strip_rows
    own_rows = first_row + jnp.arange(strip_rows, dtype=jnp.int32)
    own_samples = lax.axis_index("strip") * local_samples + jnp.arange(
        local_samples, dtype=jnp.int32
    )
    columns = column_table(spectra.shape[2] // 2, COLS)
    table = row_table(own_rows, KR, ROWS)
    passes = (WIN - 2 + sub_dev) // sub_dev
    shifted_local = apply_phase(
        jnp.einsum("skc,cn->skn", spectra, columns, preferred_element_type=jnp.float32),
        offsets,
        own_samples,
    )
    summed = jnp.einsum(
        "ab,bkn->akn",
        jnp.asarray(window_mask(0, sub_dev)),
        shifted_local.astype(jnp.float32),
        precision=lax.Precision.HIGHEST,
    )
    moving = shifted_local
    for block_offset in range(1, passes + 1):
        moving = from_behind(moving, "sub", -1)
        summed = summed + jnp.einsum(
            "ab,bkn->akn",
            jnp.asarray(window_mask(block_offset, sub_dev)),
            moving.astype(jnp.float32),
            precision=lax.Precision.HIGHEST,
        )
    table_wide = table.astype(jnp.float32)
    product = jnp.einsum(
        "mk,skn->smn",
        table_wide,
        lax.all_gather(summed, "strip", axis=1, tiled=True),
        precision=lax.Precision.HIGHEST,
    )
    frames = combine_parts(product, strip_rows)
    real_part = frames[:, :, :COLS]
    imag_part = frames[:, :, COLS:]
    log_power = jnp.log(1.0 + real_part * real_part + imag_part * imag_part)
    padded = extended(log_power, (("strip", 1),), 1)
    padded = jnp.pad(padded, ((0, 0), (0, 0), (1, 1)))
    total = jnp.zeros_like(log_power)
    for row_step in range(3):
        for col_step in range(3):
            total = total + padded[:, row_step : row_step + strip_rows, col_step : col_step + COLS]
    filtered = total / 9.0
    return remove_background(
        lax.all_to_all(filtered, "sub", split_axis=2, concat_axis=0, tiled=True)
    )


def solution(mesh):
    in_specs = (P("sub", "strip", None), P("sub"))
    out_specs = P("strip", "sub", None)
    return jax.shard_map(body, mesh=mesh, in_specs=in_specs, out_specs=out_specs, check_vma=False)
```

profile of v0, /device:TPU:0, one launch (start us, length us, event | category | flops | bytes accessed | tf_op | source)
XLA Modules:
  0.0 140.3 jit_solution(7064883153234936964)
XLA Ops:
  6.5 0.0 copy-start
  6.5 0.0 all-gather.2.cloned.1.call-start
  6.5 4.0 %fusion.26 = bf16[1024,256]{0,1:T(8,128)(2,1)S(1)} fusion(), kind=kLoop, calls=%fused_computation.51 | loop fusion | flops 4456448 | bytes 524288 | tf_op jit(solution)/shard_map/convert.9
  10.5 4.3 %negate_convert_fusion = (bf16[1024,256]{0,1:T(8,128)(2,1)S(1)}, bf16[1024,256]{0,1:T(8,128)(2,1)S(1)}) fusion(), kind=kLoop, calls=%fused_computation.42 | loop fusion | flops 5242880 | bytes 1048576 | tf_op jit(solution)/shard_map/convert.6
  14.9 0.8 fusion.60
  15.6 0.0 copy-done
  15.6 0.0 copy-start.2
  15.7 0.7 fusion.8
  16.4 0.1 subtract_convert_fusion
  16.5 5.5 %collective-permute-start = (bf16[2,128,512]{1,2,0:T(8,128)(2,1)S(1)}, bf16[2,128,512]{1,2,0:T(8,128)(2,1)S(1)}, u32[]{:S(2)}, u32[]{:S(2)}) collective-permute-start(bf16[2,128,512]{1,2,0:T(8,128)(2,1)S(1)} %pad_maximum_fusion.2), channel_id=1, source_target_pairs={{0,30},{2,0},{4,2},{6,4},{8,6},{10,8},{12,10},{14,12},{16,14},{18,... | collective-permute-start | bytes 786440 | tf_op jit(solution)/shard_map/ppermute | solution.py:19
  22.1 3.9 %collective-permute-done = bf16[2,128,512]{1,2,0:T(8,128)(2,1)S(1)} collective-permute-done((bf16[2,128,512]{1,2,0:T(8,128)(2,1)S(1)}, bf16[2,128,512]{1,2,0:T(8,128)(2,1)S(1)}, u32[]{:S(2)}, u32[]{:S(2)}) %collective-permute-start) | collective-permute-done | bytes 262176 | tf_op jit(solution)/shard_map/ppermute | solution.py:19
  25.9 4.6 %collective-permute-start.1 = (bf16[2,128,512]{1,2,0:T(8,128)(2,1)S(1)}, bf16[2,128,512]{1,2,0:T(8,128)(2,1)S(1)}, u32[]{:S(2)}, u32[]{:S(2)}) collective-permute-start(bf16[2,128,512]{1,2,0:T(8,128)(2,1)S(1)} %collective-permute-done), channel_id=1, source_target_pairs={{0,30},{2,0},{4,2},{6,4},{8,6},{10,8},{12,10},{14,12},{16,14},{18,... | collective-permute-start | bytes 786440 | tf_op jit(solution)/shard_map/ppermute | solution.py:19
  30.5 0.2 copy.11
  30.7 3.7 %collective-permute-done.1 = bf16[2,128,512]{1,2,0:T(8,128)(2,1)S(1)} collective-permute-done((bf16[2,128,512]{1,2,0:T(8,128)(2,1)S(1)}, bf16[2,128,512]{1,2,0:T(8,128)(2,1)S(1)}, u32[]{:S(2)}, u32[]{:S(2)}) %collective-permute-start.1) | collective-permute-done | bytes 262176 | tf_op jit(solution)/shard_map/ppermute | solution.py:19
  34.4 4.6 %collective-permute-start.2 = (bf16[2,128,512]{1,2,0:T(8,128)(2,1)S(1)}, bf16[2,128,512]{1,2,0:T(8,128)(2,1)S(1)}, u32[]{:S(2)}, u32[]{:S(2)}) collective-permute-start(bf16[2,128,512]{1,2,0:T(8,128)(2,1)S(1)} %collective-permute-done.1), channel_id=1, source_target_pairs={{0,30},{2,0},{4,2},{6,4},{8,6},{10,8},{12,10},{14,12},{16,14},{18,... | collective-permute-start | bytes 786440 | tf_op jit(solution)/shard_map/ppermute | solution.py:19
  39.0 0.0 copy-done.2
  39.0 1.0 fusion.74
  40.0 0.2 copy.12
  40.3 0.2 copy.13
  40.5 1.0 fusion.57
  41.4 0.2 copy.14
  41.7 0.2 copy.15
  41.9 1.1 collective-permute-done.2
  42.9 4.6 %collective-permute-start.3 = (bf16[2,128,512]{1,2,0:T(8,128)(2,1)S(1)}, bf16[2,128,512]{1,2,0:T(8,128)(2,1)}, u32[]{:S(2)}, u32[]{:S(2)}) collective-permute-start(bf16[2,128,512]{1,2,0:T(8,128)(2,1)S(1)} %collective-permute-done.2), channel_id=1, source_target_pairs={{0,30},{2,0},{4,2},{6,4},{8,6},{10,8},{12,10},{14,12},{16,14},{18,... | collective-permute-start | bytes 786440 | tf_op jit(solution)/shard_map/ppermute | solution.py:19
  47.5 1.0 fusion.55
  48.5 0.0 copy-start.1
  48.5 0.2 copy.16
  48.8 0.2 copy.17
  48.9 1.8 %fusion.53 = f32[128,512,2]{1,2,0:T(2,128)} fusion(bf16[2,128,512]{2,0,1:T(2,128)(2,1)S(1)} %copy.17), kind=kOutput, calls=%fused_computation.98 | convolution fusion | flops 3145728 | bytes 786432 | tf_op jit(solution)/shard_map/ab,bkn->akn/dot_general | solution.py:124
  50.7 1.2 copy.18
  52.0 0.0 collective-permute-done.3
  52.0 1.1 copy.19
  53.1 0.0 copy-done.1
  53.1 1.8 %fusion.75 = f32[128,512,2]{1,2,0:T(2,128)} fusion(bf16[2,128,512]{2,0,1:T(2,128)(2,1)S(1)} %copy.19, f32[2,2,1]{1,0,2:T(2,128)S(1)} %copy-done.1), kind=kOutput, calls=%fused_computation.120 | convolution fusion | flops 3145728 | bytes 786448 | tf_op jit(solution)/shard_map/ab,bkn->akn/dot_general | solution.py:124
  54.9 2.0 %copy.20 = f32[128,512,2]{0,1,2:T(8,128)} copy(f32[128,512,2]{1,2,0:T(2,128)} %fusion.75) | data formatting | bytes 1048576 | tf_op jit(solution)/shard_map/ab,bkn->akn/dot_general | solution.py:124
  56.9 2.0 %add_bitcast_fusion = f32[2,128,512]{1,2,0:T(8,128)} fusion(f32[128,512,2]{0,1,2:T(8,128)} %copy.20, f32[128,512,2]{0,1,2:T(8,128)S(1)} %copy.18, f32[128,512,2]{0,1,2:T(8,128)S(1)} %copy.16, f32[128,512,2]{0,1,2:T(8,128)S(1)} %copy.12, f32[128,512,2]{0,1,2:T(8,128)S(1)} %copy.14), kind=kLoop, calls=%fused_computation.62 | loop fusion | flops 524288 | bytes 3145728 | tf_op jit(solution)/shard_map/add | solution.py:124
  58.9 0.0 all-gather.2.cloned.1.call-update
  58.9 2.5 %multiply_convert_fusion.2 = (bf16[512,256]{1,0:T(8,128)(2,1)S(1)}, bf16[512,256]{1,0:T(8,128)(2,1)S(1)}) fusion(s32[256]{0:T(256)S(1)} %iota_add_fusion.1, s32[512]{0:T(512)S(1)} %iota_add_fusion), kind=kLoop, calls=%fused_computation.61 | loop fusion | flops 2359296 | bytes 527360 | tf_op jit(solution)/shard_map/convert
  61.4 19.7 %all-gather.2.cloned.1.call-done = f32[2,256,512]{1,2,0:T(8,128)} async-done(((f32[2,128,512]{1,2,0:T(8,128)}), f32[2,256,512]{1,2,0:T(8,128)}) %all-gather.2.cloned.1.call-update) | async-done | bytes 1048592 | tf_op jit(solution)/shard_map/all_gather | solution.py:134
  81.2 3.1 %convolution_bitcast_fusion = f32[2,1024,512]{1,2,0:T(8,128)S(1)} fusion(f32[2,256,512]{1,2,0:T(8,128)} %all-gather.2.cloned.1.call-done, bf16[512,256]{1,0:T(8,128)(2,1)S(1)} %get-tuple-element.10, bf16[512,256]{1,0:T(8,128)(2,1)S(1)} %get-tuple-element.9), kind=kOutput, calls=%fused_computation | convolution fusion | flops 3222274048 | bytes 5767168 | tf_op jit(solution)/shard_map/mk,skn->smn/dot_general | solution.py:131
  84.3 0.5 fusion.18
  84.8 0.1 fusion.73
  85.0 2.3 %collective-permute-start.4 = (f32[2,1,256]{1,2,0:T(8,128)S(1)}, f32[2,1,256]{1,2,0:T(8,128)S(1)}, u32[]{:S(2)}, u32[]{:S(2)}) collective-permute-start(f32[2,1,256]{1,2,0:T(8,128)S(1)} %get-tuple-element.5), channel_id=1, source_target_pairs={{0,1},{2,3},{4,5},{6,7},{8,9},{10,11},{12,13},{14,15},{16,17},{18,... | collective-permute-start | bytes 6152 | tf_op jit(solution)/shard_map/ppermute | solution.py:29
  87.2 1.3 collective-permute-start.5
  88.5 4.2 %collective-permute-done.4 = f32[2,1,256]{1,2,0:T(8,128)S(1)} collective-permute-done((f32[2,1,256]{1,2,0:T(8,128)S(1)}, f32[2,1,256]{1,2,0:T(8,128)S(1)}, u32[]{:S(2)}, u32[]{:S(2)}) %collective-permute-start.4) | collective-permute-done | bytes 2080 | tf_op jit(solution)/shard_map/ppermute | solution.py:29
  92.8 4.1 %collective-permute-done.5 = f32[2,1,256]{1,2,0:T(8,128)S(1)} collective-permute-done((f32[2,1,256]{1,2,0:T(8,128)S(1)}, f32[2,1,256]{1,2,0:T(8,128)S(1)}, u32[]{:S(2)}, u32[]{:S(2)}) %collective-permute-start.5) | collective-permute-done | bytes 2080 | tf_op jit(solution)/shard_map/ppermute | solution.py:30
  96.9 0.5 select_maximum_fusion
  97.4 1.8 %fusion.12 = f32[2,512,256]{1,2,0:T(8,128)S(1)} fusion(f32[2,514,258]{1,2,0:T(8,128)S(1)} %select_maximum_fusion, f32[2,1,256]{1,2,0:T(8,128)S(1)} %collective-permute-done.5, f32[2,512,256]{1,2,0:T(8,128)S(1)} %fusion.18, f32[2,1,256]{1,2,0:T(8,128)S(1)} %collective-permute-done.4), kind=kLoop, calls=%fused_computation.22 | loop fusion | flops 2883584 | bytes 8392704 | tf_op jit(solution)/shard_map/div | solution.py:147
  99.2 0.8 copy.9
  100.0 30.1 %all_to_all.18 = f32[2,512,256]{1,0,2:T(2,128)S(1)} all-to-all(f32[2,512,256]{1,0,2:T(2,128)S(1)} %copy.9), channel_id=1, replica_groups=mesh['sub'=16,'strip'=2] {'sub'}, dimensions={2} | all-to-all | bytes 2097152 | tf_op jit(solution)/shard_map/all_to_all | solution.py:149
  130.2 0.5 copy.22
  130.7 0.7 all_to_all.16
  131.4 2.0 %fusion.21 = f32[512,16,32]{0,2,1:T(8,128)} fusion(f32[32,512,16]{1,0,2:T(8,128)S(1)} %all_to_all.16), kind=kOutput, calls=%fused_computation.39 | convolution fusion | flops 100680704 | bytes 2097152 | tf_op jit(solution)/shard_map/rcg,gf->rcf/dot_general | solution.py:95
  (4 shorter events, 0.0 us)
Async XLA Ops:
  6.5 9.1 %copy-start = (bf16[2,128,2048]{2,1,0:T(8,128)(2,1)S(1)}, bf16[2,128,2048]{2,1,0:T(8,128)(2,1)}, u32[]{:S(2)}) copy-start(bf16[2,128,2048]{2,1,0:T(8,128)(2,1)} %param.7) | copy-start | bytes 3145732
  6.5 74.7 %all-gather.2.cloned.1.call-start = ((), (), s32[]{:S(2)}) async-start(), calls=%async_computation.1 | async-start | bytes 1572864 | tf_op jit(solution)/shard_map/all_gather | solution.py:134
  15.6 23.4 %copy-start.2 = (f32[2,2,1]{1,0,2:T(2,128)S(1)}, f32[2,2,1]{1,0,2:T(2,128)}, u32[]{:S(2)}) copy-start(f32[2,2,1]{1,0,2:T(2,128)} %constant.94) | copy-start | bytes 52
  16.5 9.4 %collective-permute-start = (bf16[2,128,512]{1,2,0:T(8,128)(2,1)S(1)}, bf16[2,128,512]{1,2,0:T(8,128)(2,1)S(1)}, u32[]{:S(2)}, u32[]{:S(2)}) collective-permute-start(bf16[2,128,512]{1,2,0:T(8,128)(2,1)S(1)} %pad_maximum_fusion.2), channel_id=1, source_target_pairs={{0,30},{2,0},{4,2},{6,4},{8,6},{10,8},{12,10},{14,12},{16,14},{18,... | collective-permute-start | bytes 786440 | tf_op jit(solution)/shard_map/ppermute | solution.py:19
  25.9 8.5 %collective-permute-start.1 = (bf16[2,128,512]{1,2,0:T(8,128)(2,1)S(1)}, bf16[2,128,512]{1,2,0:T(8,128)(2,1)S(1)}, u32[]{:S(2)}, u32[]{:S(2)}) collective-permute-start(bf16[2,128,512]{1,2,0:T(8,128)(2,1)S(1)} %collective-permute-done), channel_id=1, source_target_pairs={{0,30},{2,0},{4,2},{6,4},{8,6},{10,8},{12,10},{14,12},{16,14},{18,... | collective-permute-start | bytes 786440 | tf_op jit(solution)/shard_map/ppermute | solution.py:19
  34.4 8.5 %collective-permute-start.2 = (bf16[2,128,512]{1,2,0:T(8,128)(2,1)S(1)}, bf16[2,128,512]{1,2,0:T(8,128)(2,1)S(1)}, u32[]{:S(2)}, u32[]{:S(2)}) collective-permute-start(bf16[2,128,512]{1,2,0:T(8,128)(2,1)S(1)} %collective-permute-done.1), channel_id=1, source_target_pairs={{0,30},{2,0},{4,2},{6,4},{8,6},{10,8},{12,10},{14,12},{16,14},{18,... | collective-permute-start | bytes 786440 | tf_op jit(solution)/shard_map/ppermute | solution.py:19
  42.9 9.0 %collective-permute-start.3 = (bf16[2,128,512]{1,2,0:T(8,128)(2,1)S(1)}, bf16[2,128,512]{1,2,0:T(8,128)(2,1)}, u32[]{:S(2)}, u32[]{:S(2)}) collective-permute-start(bf16[2,128,512]{1,2,0:T(8,128)(2,1)S(1)} %collective-permute-done.2), channel_id=1, source_target_pairs={{0,30},{2,0},{4,2},{6,4},{8,6},{10,8},{12,10},{14,12},{16,14},{18,... | collective-permute-start | bytes 786440 | tf_op jit(solution)/shard_map/ppermute | solution.py:19
  48.5 4.6 %copy-start.1 = (f32[2,2,1]{1,0,2:T(2,128)S(1)}, f32[2,2,1]{1,0,2:T(2,128)}, u32[]{:S(2)}) copy-start(f32[2,2,1]{1,0,2:T(2,128)} %constant.95) | copy-start | bytes 52
  85.0 7.8 %collective-permute-start.4 = (f32[2,1,256]{1,2,0:T(8,128)S(1)}, f32[2,1,256]{1,2,0:T(8,128)S(1)}, u32[]{:S(2)}, u32[]{:S(2)}) collective-permute-start(f32[2,1,256]{1,2,0:T(8,128)S(1)} %get-tuple-element.5), channel_id=1, source_target_pairs={{0,1},{2,3},{4,5},{6,7},{8,9},{10,11},{12,13},{14,15},{16,17},{18,... | collective-permute-start | bytes 6152 | tf_op jit(solution)/shard_map/ppermute | solution.py:29
  87.2 9.7 %collective-permute-start.5 = (f32[2,1,256]{1,2,0:T(8,128)S(1)}, f32[2,1,256]{1,2,0:T(8,128)S(1)}, u32[]{:S(2)}, u32[]{:S(2)}) collective-permute-start(f32[2,1,256]{1,2,0:T(8,128)S(1)} %get-tuple-element.6), channel_id=1, source_target_pairs={{1,0},{3,2},{5,4},{7,6},{9,8},{11,10},{13,12},{15,14},{17,16},{19,... | collective-permute-start | bytes 6152 | tf_op jit(solution)/shard_map/ppermute | solution.py:30
Sparse Core Ops, SparseCore 0:
  59.0 22.1 all-gather.1
where the time goes:
time: 141 us; the launch traced here: 140 us
  waiting for transfers between devices  36.8 us (26%)
  blocking collectives  30.1 us (21%)
  starting transfers between devices  22.9 us (16%)
  other arithmetic  16.4 us (12%)
  between operations  13.7 us (10%)
  matrix products  12.3 us (9%)
  local copies, waits for them, and re-layouts  8.09 us (6%)
    all_to_all x1, blocking collectives, body(): lax.all_to_all(filtered, 'sub', split_axis=2, concat_axis=0, tiled=True)  30.1 us
    all_gather x1, waiting for transfers between devices, body(): lax.all_gather(summed, 'strip', axis=1, tiled=True)  19.7 us
    ppermute x4, starting transfers between devices, from_behind(): return lax.ppermute(value, axis, pairs)  19.3 us
    another operation x4, other arithmetic  10.9 us
    ppermute x4, waiting for transfers between devices, from_behind(): return lax.ppermute(value, axis, pairs)  8.67 us
    dot_general x4, matrix products, body(): jnp.einsum('ab,bkn->akn', jnp.asarray(window_mask(block_offset, sub_dev))...  5.45 us
    ppermute x1, waiting for transfers between devices, extended(): before = lax.ppermute(last, axis, up)  4.24 us
    ppermute x1, waiting for transfers between devices, extended(): after = lax.ppermute(leading, axis, down)  4.13 us
  transfers between devices with their start and end apart: 7, of which 6 were waited for; matrix products, arithmetic and copies ran while one was open for 7% of the time, Pallas kernels for 0%

commit v1 on v0

v1 whole, which is shorter than its diff:
```python
import math

import jax
import jax.numpy as jnp
import numpy as np
from jax import lax
from jax.sharding import PartitionSpec as P

KR = 256
ROWS = 1024
COLS = 256
WIN = 8
BG = 16


def column_table(samples, parts):
    wide = COLS // parts + 2
    column = (np.arange(parts) * (wide - 2))[:, None] + np.arange(-1, wide - 1)[None, :]
    inside = (column >= 0) & (column < COLS)
    phase = ((np.arange(samples)[:, None, None] * column[None]) % samples) * (2.0 * math.pi / samples)
    cosine = np.where(inside, np.cos(phase), 0.0) / math.sqrt(samples)
    sine = np.where(inside, -np.sin(phase), 0.0) / math.sqrt(samples)
    upper = np.stack([cosine, sine], axis=2)
    lower = np.stack([-sine, cosine], axis=2)
    return jnp.asarray(np.concatenate([upper, lower], axis=0).astype(np.float32)).astype(jnp.bfloat16)


def row_table(rows):
    sample = jnp.arange(KR, dtype=jnp.int32)[:, None] - KR // 2
    phase = jnp.mod(rows[None, :] * sample, ROWS).astype(jnp.float32) * (2.0 * math.pi / ROWS)
    scale = jnp.where((rows >= 0) & (rows < ROWS), 1.0 / math.sqrt(KR), 0.0)[None, :]
    cosine = jnp.cos(phase) * scale
    sine = jnp.sin(phase) * scale
    upper = jnp.stack([cosine, sine], axis=1)
    lower = jnp.stack([-sine, cosine], axis=1)
    return jnp.concatenate([upper, lower], axis=0).astype(jnp.bfloat16)


def rotation(offsets, samples):
    angle = jnp.mod(offsets[:, None] * (samples[None, :] - KR // 2), ROWS).astype(jnp.float32) * (2.0 * math.pi / ROWS)
    return jnp.cos(angle), jnp.sin(angle)


def plain_body(spectra, offsets):
    own, depth = spectra.shape[:2]
    parts, strips = lax.axis_size("sub"), lax.axis_size("strip")
    wide = COLS // parts + 2
    high = ROWS // strips
    strip = lax.axis_index("strip")
    frames = own * parts
    table = column_table(spectra.shape[2] // 2, parts)
    cosine, sine = rotation(offsets, strip * depth + jnp.arange(depth, dtype=jnp.int32))
    mixed = jnp.einsum("skc,cdpn->dspnk", spectra, table, preferred_element_type=jnp.float32)
    real, imag = mixed[:, :, 0], mixed[:, :, 1]
    cosine, sine = cosine[None, :, None, :], sine[None, :, None, :]
    shifted = jnp.stack([real * cosine - imag * sine, real * sine + imag * cosine], axis=2).astype(jnp.bfloat16)
    held = lax.all_to_all(shifted, "sub", split_axis=0, concat_axis=0, tiled=True)
    held = held.reshape(frames, 2, wide, depth)
    whole = jnp.zeros((frames, 2, wide, strips, depth), jnp.bfloat16)
    for step in range(strips):
        part = held
        if step:
            part = lax.ppermute(held, "strip", [(i, (i + step) % strips) for i in range(strips)])
        source = jnp.mod(strip - step, strips)
        whole = lax.dynamic_update_slice(whole, part[:, :, :, None], (0, 0, 0, source, 0))
    wider = whole.reshape(frames, 2, wide, KR).astype(jnp.float32)
    summed = wider
    for lead in range(1, WIN):
        summed = summed + jnp.roll(wider, -lead, axis=0)
    rows = strip * high + jnp.arange(-1, high + 1, dtype=jnp.int32)
    product = jnp.einsum(
        "fpnk,pkqm->qnfm",
        summed.astype(jnp.bfloat16),
        row_table(rows).reshape(2, KR, 2, high + 2),
        preferred_element_type=jnp.float32,
    )
    log_power = jnp.log(1.0 + product[0] * product[0] + product[1] * product[1])
    total = log_power[:, :, :-2] + log_power[:, :, 1:-1] + log_power[:, :, 2:]
    filtered = (total[:-2] + total[1:-1] + total[2:]) / 9.0
    background = filtered
    for behind in range(1, BG):
        background = background + jnp.roll(filtered, behind, axis=1)
    return jnp.transpose(filtered - background / BG, (2, 0, 1))


def solution(mesh):
    in_specs = (P("sub", "strip", None), P("sub"))
    out_specs = P("strip", "sub", None)
    return jax.shard_map(plain_body, mesh=mesh, in_specs=in_specs, out_specs=out_specs, check_vma=False)
```

time: 141 us -> 123 us (0.87)
  local copies, waits for them, and re-layouts: 8.09 us -> 85.5 us
  blocking collectives: 30.1 us -> 0 us
  waiting for transfers between devices: 36.8 us -> 10.5 us
  starting transfers between devices: 22.9 us -> 8.96 us
  between operations: 13.7 us -> 0.49 us
  other arithmetic: 16.4 us -> 9.46 us
  matrix products: 12.3 us -> 7.94 us
    slice x1 -> x64, local copies, waits for them, and re-layouts: 0.14 us -> 52.2 us  [the longest x41 51.1 us: plain_body(): summed = summed + jnp.roll(wider, -lead, axis=0)]
    all_to_all x1 -> x0, blocking collectives: 30.1 us -> none  [body(): lax.all_to_all(filtered, 'sub', split_axis=2, concat_axis=0, tiled=True)]
    dynamic_update_slice x0 -> x2, local copies, waits for them, and re-layouts: none -> 26.1 us  [plain_body(): lax.dynamic_update_slice(whole, part[:, :, :, None], (0, 0, 0, source, 0))]
    ppermute x6 -> x1, starting transfers between devices: 22.9 us -> 1.55 us  [plain_body(): lax.ppermute(held, 'strip', [(i, (i + step) % strips) for i in range(stri...]
    all_gather x1 -> x0, waiting for transfers between devices: 19.7 us -> none  [body(): lax.all_gather(summed, 'strip', axis=1, tiled=True)]
    ppermute x6 -> x1, waiting for transfers between devices: 17 us -> 0.01 us  [plain_body(): lax.ppermute(held, 'strip', [(i, (i + step) % strips) for i in range(stri...]
    all_to_all x0 -> x1, waiting for transfers between devices: none -> 10.5 us  [plain_body(): lax.all_to_all(shifted, 'sub', split_axis=0, concat_axis=0, tiled=True)]
    another operation x4 -> x3, other arithmetic: 10.9 us -> 2.49 us
  transfers between devices with their start and end apart: 7 -> 2, of which waited for: 6 -> 1; matrix products, arithmetic and copies ran while one was open for 7% -> 14% of each run, Pallas kernels for 0% -> 0%
where the time goes in v1:
time: 123 us
  local copies, waits for them, and re-layouts  85.5 us (70%)
  waiting for transfers between devices  10.5 us (9%)
  other arithmetic  9.46 us (8%)
  starting transfers between devices  8.96 us (7%)
  matrix products  7.94 us (6%)
    slice x41, local copies, waits for them, and re-layouts, plain_body(): summed = summed + jnp.roll(wider, -lead, axis=0)  51.1 us
    dynamic_update_slice x2, local copies, waits for them, and re-layouts, plain_body(): lax.dynamic_update_slice(whole, part[:, :, :, None], (0, 0, 0, source, 0))  26.1 us
    all_to_all x1, waiting for transfers between devices, plain_body(): lax.all_to_all(shifted, 'sub', split_axis=0, concat_axis=0, tiled=True)  10.5 us
    all_to_all x1, starting transfers between devices, plain_body(): lax.all_to_all(shifted, 'sub', split_axis=0, concat_axis=0, tiled=True)  7.41 us
    dot_general x1, matrix products, plain_body(): jnp.einsum('fpnk,pkqm->qnfm', summed.astype(jnp.bfloat16), row_table(rows...  5.03 us
    transpose x1, other arithmetic, plain_body(): return jnp.transpose(filtered - background / BG, (2, 0, 1))  4.87 us
    dot_general x1, matrix products, plain_body(): jnp.einsum('skc,cdpn->dspnk', spectra, table, preferred_element_type=jnp....  2.91 us
  transfers between devices with their start and end apart: 2, of which 1 were waited for; matrix products, arithmetic and copies ran while one was open for 14% of the time, Pallas kernels for 0%

profile of v1, /device:TPU:0, one launch (start us, length us, event | category | flops | bytes accessed | tf_op | source)
XLA Modules:
  0.0 122.8 jit_solution(18129780163678179763)
XLA Ops:
  0.0 0.9 fusion.41
  0.9 0.4 copy-done
  1.2 2.9 %convolution_bitcast_fusion.1 = f32[16,2,2,18,128]{4,3,1,2,0:T(8,128)S(1)} fusion(bf16[2048,16,2,18,1]{0,3,4,2,1:T(8,128)(2,1)} %constant.81, bf16[2,128,2048]{2,1,0:T(8,128)(2,1)S(1)} %copy-done), kind=kOutput, calls=%fused_computation.7 | convolution fusion | flops 603979776 | bytes 3997696 | tf_op jit(solution)/shard_map/skc,cdpn->dspnk/dot_general | solution.py:53
  4.2 0.1 subtract_convert_fusion
  4.3 0.9 copy.25
  5.3 7.4 %all-to-all-start = ((bf16[16,2,2,18,128]{4,2,3,1,0:T(2,128)(2,1)}), bf16[16,2,2,18,128]{4,2,3,1,0:T(2,128)(2,1)S(1)}, u32[]{:S(2)}, u32[]{:S(2)}) async-start(bf16[16,2,2,18,128]{4,2,3,1,0:T(2,128)(2,1)} %copy.25), calls=%async_computation | async-start | bytes 589824 | tf_op jit(solution)/shard_map/all_to_all | solution.py:57
  12.8 10.5 %all-to-all-done = bf16[16,2,2,18,128]{4,2,3,1,0:T(2,128)(2,1)S(1)} async-done(((bf16[16,2,2,18,128]{4,2,3,1,0:T(2,128)(2,1)}), bf16[16,2,2,18,128]{4,2,3,1,0:T(2,128)(2,1)S(1)}, u32[]{:S(2)}, u32[]{:S(2)}) %all-to-all-start) | async-done | bytes 294944 | tf_op jit(solution)/shard_map/all_to_all | solution.py:57
  23.2 0.2 copy.28
  23.5 1.6 %collective-permute-start = (bf16[32,2,18,128]{3,0,2,1:T(8,128)(2,1)S(1)}, bf16[32,2,18,128]{3,0,2,1:T(8,128)(2,1)S(1)}, u32[]{:S(2)}, u32[]{:S(2)}) collective-permute-start(bf16[32,2,18,128]{3,0,2,1:T(8,128)(2,1)S(1)} %bitcast.75), channel_id=1, source_target_pairs={{0,1},{1,0},{2,3},{3,2},{4,5},{5,4},{6,7},{7,6},{8,9},{9,8},{10,11... | collective-permute-start | bytes 884744 | tf_op jit(solution)/shard_map/ppermute | solution.py:63
  25.0 2.3 %fusion.36 = (bf16[256,1,514]{0,2,1:T(8,128)(2,1)S(1)}, bf16[256,1,514]{0,2,1:T(8,128)(2,1)S(1)}, bf16[256,1,514]{0,2,1:T(8,128)(2,1)S(1)}) fusion(f32[514]{0:T(1024)S(1)} %and_select_fusion, s32[256]{0:T(256)S(1)} %iota_add_fusion, s32[514]{0:T(1024)S(1)} %add_add_fusion), kind=kLoop, calls=%fused_computation.55 | loop fusion | flops 2631680 | bytes 794640 | tf_op jit(solution)/shard_map/convert.7
  27.4 0.1 maximum_maximum_fusion
  27.5 1.1 convert_element_type.47
  28.6 0.6 copy.27
  29.2 0.3 broadcast_in_dim.23
  29.5 13.0 %dynamic_update_slice.6 = bf16[32,2,18,2,128]{4,3,1,2,0:T(2,128)(2,1)S(1)} dynamic-update-slice(bf16[32,2,18,2,128]{4,3,1,2,0:T(2,128)(2,1)S(1)} %broadcast_in_dim.23, bf16[32,2,18,1,128]{4,3,1,2,0:T(2,128)(2,1)S(1)} %copy.27, s32[]{:T(128)} %constant.65.clone.1, s32[]{:T(128)} %constant.65.clone.1, s32[]{:T(128)} %constant.65.clone.1, s32[]{:T(128)S(6)} %select_n.63, s32[]{:T(128)} %constant.65.clone.1) | dynamic-update-slice | bytes 589828 | tf_op jit(solution)/shard_map/dynamic_update_slice | solution.py:65
  42.5 0.5 copy.29
  43.0 13.1 %dynamic_update_slice.7 = bf16[32,2,18,2,128]{4,3,1,2,0:T(2,128)(2,1)S(1)} dynamic-update-slice(bf16[32,2,18,2,128]{4,3,1,2,0:T(2,128)(2,1)S(1)} %dynamic_update_slice.6, bf16[32,2,18,1,128]{4,3,1,2,0:T(2,128)(2,1)S(1)} %copy.29, s32[]{:T(128)} %constant.65.clone.1, s32[]{:T(128)} %constant.65.clone.1, s32[]{:T(128)} %constant.65.clone.1, s32[]{:T(128)S(6)} %select_n.65, s32[]{:T(128)} %constant.65.clone.1) | dynamic-update-slice | bytes 589828 | tf_op jit(solution)/shard_map/dynamic_update_slice | solution.py:65
  56.1 0.6 slice.321
  56.9 0.1 slice.329
  57.0 0.8 slice.331
  57.7 0.1 slice.333
  57.8 1.3 %slice.332 = f32[25,2,18,2,128]{4,3,1,2,0:T(2,128)} slice(bf16[32,2,18,2,128]{4,3,1,2,0:T(2,128)(2,1)S(1)} %dynamic_update_slice.7), slice={[7:32], [0:2], [0:18], [0:2], [0:128]} | slice | bytes 1843200 | tf_op jit(solution)/shard_map/jit(_roll_static)/slice | solution.py:69
  59.1 1.3 %slice.330 = f32[26,2,18,2,128]{4,3,1,2,0:T(2,128)} slice(bf16[32,2,18,2,128]{4,3,1,2,0:T(2,128)(2,1)S(1)} %dynamic_update_slice.7), slice={[6:32], [0:2], [0:18], [0:2], [0:128]} | slice | bytes 1916928 | tf_op jit(solution)/shard_map/jit(_roll_static)/slice | solution.py:69
  60.4 1.4 %slice.328 = f32[27,2,18,2,128]{4,3,1,2,0:T(2,128)} slice(bf16[32,2,18,2,128]{4,3,1,2,0:T(2,128)(2,1)S(1)} %dynamic_update_slice.7), slice={[5:32], [0:2], [0:18], [0:2], [0:128]} | slice | bytes 1990656 | tf_op jit(solution)/shard_map/jit(_roll_static)/slice | solution.py:69
  61.7 1.3 %slice.326 = f32[28,2,18,2,128]{4,3,1,2,0:T(2,128)} slice(bf16[32,2,18,2,128]{4,3,1,2,0:T(2,128)(2,1)S(1)} %dynamic_update_slice.7), slice={[4:32], [0:2], [0:18], [0:2], [0:128]} | slice | bytes 2064384 | tf_op jit(solution)/shard_map/jit(_roll_static)/slice | solution.py:69
  63.1 1.4 %slice.324 = f32[29,2,18,2,128]{4,3,1,2,0:T(2,128)} slice(bf16[32,2,18,2,128]{4,3,1,2,0:T(2,128)(2,1)S(1)} %dynamic_update_slice.7), slice={[3:32], [0:2], [0:18], [0:2], [0:128]} | slice | bytes 2138112 | tf_op jit(solution)/shard_map/jit(_roll_static)/slice | solution.py:69
  64.4 1.4 %slice.322 = f32[30,2,18,2,128]{4,3,1,2,0:T(2,128)} slice(bf16[32,2,18,2,128]{4,3,1,2,0:T(2,128)(2,1)S(1)} %dynamic_update_slice.7), slice={[2:32], [0:2], [0:18], [0:2], [0:128]} | slice | bytes 2211840 | tf_op jit(solution)/shard_map/jit(_roll_static)/slice | solution.py:69
  65.8 0.4 slice.320
  66.2 1.8 %reshape.339 = f32[32,2,18,256]{3,1,2,0:T(2,128)} reshape(bf16[32,2,18,2,128]{4,3,1,2,0:T(2,128)(2,1)S(1)} %dynamic_update_slice.7) | data formatting | bytes 1769472 | tf_op jit(solution)/shard_map/convert_element_type | solution.py:66
  68.0 1.4 %copy.32 = f32[1,2,18,2,128]{4,3,2,1,0:T(2,128)} copy(f32[1,2,18,2,128]{4,3,1,2,0:T(2,128)} %slice.321) | data formatting | bytes 73728 | tf_op jit(solution)/shard_map/jit(_roll_static)/slice | solution.py:69
  69.4 0.1 reshape.341
  69.5 0.7 copy.57
  70.1 0.1 slice.263
  70.3 0.7 copy.36
  71.0 0.2 reshape.342
  71.1 0.7 copy.58
  71.8 0.2 slice.271
  72.1 0.8 copy.40
  72.9 1.9 %slice.275 = f32[6,2,18,256]{3,1,2,0:T(2,128)} reshape(f32[6,2,18,2,128]{4,3,1,2,0:T(2,128)} %slice.331) | data formatting | bytes 442368 | tf_op jit(solution)/shard_map/jit(_roll_static)/slice | solution.py:69
  74.7 1.7 %copy.42 = f32[6,2,18,256]{3,0,2,1:T(8,128)} copy(f32[6,2,18,256]{3,1,2,0:T(2,128)} %slice.275) | data formatting | bytes 442368 | tf_op jit(solution)/shard_map/jit(_roll_static)/slice | solution.py:69
  76.4 1.0 slice.279
  77.4 1.7 %copy.44 = f32[7,2,18,256]{3,0,2,1:T(8,128)} copy(f32[7,2,18,256]{3,1,2,0:T(2,128)} %slice.279) | data formatting | bytes 516096 | tf_op jit(solution)/shard_map/jit(_roll_static)/slice | solution.py:69
  79.2 2.0 %slice.277 = f32[25,2,18,256]{3,1,2,0:T(2,128)} reshape(f32[25,2,18,2,128]{4,3,1,2,0:T(2,128)S(1)} %copy-done.6) | data formatting | bytes 1843200 | tf_op jit(solution)/shard_map/jit(_roll_static)/slice | solution.py:69
  81.2 2.5 %copy.43 = f32[25,2,18,256]{3,0,2,1:T(8,128)} copy(f32[25,2,18,256]{3,1,2,0:T(2,128)} %slice.277) | data formatting | bytes 1843200 | tf_op jit(solution)/shard_map/jit(_roll_static)/slice | solution.py:69
  83.6 2.0 %slice.273 = f32[26,2,18,256]{3,1,2,0:T(2,128)} reshape(f32[26,2,18,2,128]{4,3,1,2,0:T(2,128)S(1)} %copy-done.5) | data formatting | bytes 1916928 | tf_op jit(solution)/shard_map/jit(_roll_static)/slice | solution.py:69
  85.7 2.5 %copy.41 = f32[26,2,18,256]{3,0,2,1:T(8,128)} copy(f32[26,2,18,256]{3,1,2,0:T(2,128)} %slice.273) | data formatting | bytes 1916928 | tf_op jit(solution)/shard_map/jit(_roll_static)/slice | solution.py:69
  88.2 2.1 %slice.269 = f32[27,2,18,256]{3,1,2,0:T(2,128)} reshape(f32[27,2,18,2,128]{4,3,1,2,0:T(2,128)S(1)} %copy-done.4) | data formatting | bytes 1990656 | tf_op jit(solution)/shard_map/jit(_roll_static)/slice | solution.py:69
  90.3 2.5 %copy.39 = f32[27,2,18,256]{3,0,2,1:T(8,128)} copy(f32[27,2,18,256]{3,1,2,0:T(2,128)} %slice.269) | data formatting | bytes 1990656 | tf_op jit(solution)/shard_map/jit(_roll_static)/slice | solution.py:69
  92.9 2.1 %slice.265 = f32[28,2,18,256]{3,1,2,0:T(2,128)} reshape(f32[28,2,18,2,128]{4,3,1,2,0:T(2,128)S(1)} %copy-done.3) | data formatting | bytes 2064384 | tf_op jit(solution)/shard_map/jit(_roll_static)/slice | solution.py:69
  95.0 2.5 %copy.38 = f32[28,2,18,256]{3,0,2,1:T(8,128)} copy(f32[28,2,18,256]{3,1,2,0:T(2,128)} %slice.265) | data formatting | bytes 2064384 | tf_op jit(solution)/shard_map/jit(_roll_static)/slice | solution.py:69
  97.6 2.5 %slice.261 = f32[29,2,18,256]{3,1,2,0:T(2,128)} reshape(f32[29,2,18,2,128]{4,3,1,2,0:T(2,128)S(1)} %copy-done.2) | data formatting | bytes 2138112 | tf_op jit(solution)/shard_map/jit(_roll_static)/slice | solution.py:69
  100.1 2.6 %copy.35 = f32[29,2,18,256]{3,0,2,1:T(8,128)} copy(f32[29,2,18,256]{3,1,2,0:T(2,128)} %slice.261) | data formatting | bytes 2138112 | tf_op jit(solution)/shard_map/jit(_roll_static)/slice | solution.py:69
  102.7 2.4 %slice.257 = f32[30,2,18,256]{3,1,2,0:T(2,128)} reshape(f32[30,2,18,2,128]{4,3,1,2,0:T(2,128)S(1)} %copy-done.1) | data formatting | bytes 2211840 | tf_op jit(solution)/shard_map/jit(_roll_static)/slice | solution.py:69
  105.0 2.5 %copy.34 = f32[30,2,18,256]{3,0,2,1:T(8,128)} copy(f32[30,2,18,256]{3,1,2,0:T(2,128)} %slice.257) | data formatting | bytes 2211840 | tf_op jit(solution)/shard_map/jit(_roll_static)/slice | solution.py:69
  107.5 1.3 %reshape.340 = f32[31,2,18,256]{3,1,2,0:T(2,128)S(1)} reshape(f32[31,2,18,2,128]{4,3,1,2,0:T(2,128)S(1)} %slice.320) | data formatting | bytes 2285568 | tf_op jit(solution)/shard_map/jit(_roll_static)/slice | solution.py:69
  108.9 0.2 copy.56
  109.1 1.0 copy-done.7
  110.1 0.3 copy-done.8
  110.4 5.0 %convolution_bitcast_fusion = f32[2,18,32,514]{3,2,1,0:T(8,128)S(1)} fusion(bf16[2,256,2,514,1]{1,0,3,2,4:T(2,128)(2,1)S(1)} %bitcast.73, f32[1,2,18,256]{3,0,2,1:T(1,128)S(1)} %bitcast.76, f32[31,2,18,256]{3,0,2,1:T(8,128)S(1)} %copy.56, f32[2,2,18,256]{3,0,2,1:T(2,128)S(1)} %copy-done.10, f32[30,2,18,256]{3,0,2,1:T(8,128)} %copy.34, ...), kind=kOutput, calls=%fused_computation | convolution fusion | flops 610762752 | bytes 12858368 | tf_op jit(solution)/shard_map/fpnk,pkqm->qnfm/dot_general | solution.py:71
  115.5 0.3 fusion.2
  115.8 0.7 slice_add_fusion
  116.5 0.1 fusion.12
  117.4 0.1 slice.369
  118.0 4.9 %fusion.30 = f32[512,16,32]{0,2,1:T(8,128)} fusion(f32[16,17,512]{2,1,0:T(8,128)S(1)} %slice.371, f32[16,15,512]{2,1,0:T(8,128)S(1)} %slice.370, f32[16,18,512]{2,1,0:T(8,128)S(1)} %slice.369, f32[16,14,512]{2,1,0:T(8,128)S(1)} %slice.368, f32[16,19,512]{2,1,0:T(8,128)S(1)} %slice.367, f32[16,13,512]{2,1,0:T(8,128)S(1)} %slice.366, ...), kind=kLoop, calls=%fused_computation.41 | loop fusion | flops 9175040 | bytes 19922944 | tf_op jit(solution)/shard_map/transpose | solution.py:83
  (52 shorter events, 1.3 us)
Async XLA Ops:
  0.0 1.2 %copy-start = (bf16[2,128,2048]{2,1,0:T(8,128)(2,1)S(1)}, bf16[2,128,2048]{2,1,0:T(8,128)(2,1)}, u32[]{:S(2)}) copy-start(bf16[2,128,2048]{2,1,0:T(8,128)(2,1)} %param.3) | copy-start | bytes 3145732
  5.3 18.0 %all-to-all-start = ((bf16[16,2,2,18,128]{4,2,3,1,0:T(2,128)(2,1)}), bf16[16,2,2,18,128]{4,2,3,1,0:T(2,128)(2,1)S(1)}, u32[]{:S(2)}, u32[]{:S(2)}) async-start(bf16[16,2,2,18,128]{4,2,3,1,0:T(2,128)(2,1)} %copy.25), calls=%async_computation | async-start | bytes 589824 | tf_op jit(solution)/shard_map/all_to_all | solution.py:57
  23.5 19.0 %collective-permute-start = (bf16[32,2,18,128]{3,0,2,1:T(8,128)(2,1)S(1)}, bf16[32,2,18,128]{3,0,2,1:T(8,128)(2,1)S(1)}, u32[]{:S(2)}, u32[]{:S(2)}) collective-permute-start(bf16[32,2,18,128]{3,0,2,1:T(8,128)(2,1)S(1)} %bitcast.75), channel_id=1, source_target_pairs={{0,1},{1,0},{2,3},{3,2},{4,5},{5,4},{6,7},{7,6},{8,9},{9,8},{10,11... | collective-permute-start | bytes 884744 | tf_op jit(solution)/shard_map/ppermute | solution.py:63
  72.0 7.1 %copy-start.6 = (f32[25,2,18,2,128]{4,3,1,2,0:T(2,128)S(1)}, f32[25,2,18,2,128]{4,3,1,2,0:T(2,128)}, u32[]{:S(2)}) copy-start(f32[25,2,18,2,128]{4,3,1,2,0:T(2,128)} %slice.332) | copy-start | bytes 2764804
  81.2 2.5 %copy-start.5 = (f32[26,2,18,2,128]{4,3,1,2,0:T(2,128)S(1)}, f32[26,2,18,2,128]{4,3,1,2,0:T(2,128)}, u32[]{:S(2)}) copy-start(f32[26,2,18,2,128]{4,3,1,2,0:T(2,128)} %slice.330) | copy-start | bytes 2875396
  85.7 2.5 %copy-start.4 = (f32[27,2,18,2,128]{4,3,1,2,0:T(2,128)S(1)}, f32[27,2,18,2,128]{4,3,1,2,0:T(2,128)}, u32[]{:S(2)}) copy-start(f32[27,2,18,2,128]{4,3,1,2,0:T(2,128)} %slice.328) | copy-start | bytes 2985988
  90.3 2.5 %copy-start.3 = (f32[28,2,18,2,128]{4,3,1,2,0:T(2,128)S(1)}, f32[28,2,18,2,128]{4,3,1,2,0:T(2,128)}, u32[]{:S(2)}) copy-start(f32[28,2,18,2,128]{4,3,1,2,0:T(2,128)} %slice.326) | copy-start | bytes 3096580
  95.0 2.6 %copy-start.2 = (f32[29,2,18,2,128]{4,3,1,2,0:T(2,128)S(1)}, f32[29,2,18,2,128]{4,3,1,2,0:T(2,128)}, u32[]{:S(2)}) copy-start(f32[29,2,18,2,128]{4,3,1,2,0:T(2,128)} %slice.324) | copy-start | bytes 3207172
  100.0 2.6 %copy-start.1 = (f32[30,2,18,2,128]{4,3,1,2,0:T(2,128)S(1)}, f32[30,2,18,2,128]{4,3,1,2,0:T(2,128)}, u32[]{:S(2)}) copy-start(f32[30,2,18,2,128]{4,3,1,2,0:T(2,128)} %slice.322) | copy-start | bytes 3317764
  107.5 1.6 %copy-start.9 = (f32[4,2,18,256]{3,0,2,1:T(4,128)S(1)}, f32[4,2,18,256]{3,0,2,1:T(4,128)}, u32[]{:S(2)}) copy-start(f32[4,2,18,256]{3,0,2,1:T(4,128)} %copy.58) | copy-start | bytes 442372
  107.5 1.6 %copy-start.11 = (f32[1,2,18,2,128]{4,3,2,1,0:T(2,128)S(1)}, f32[1,2,18,2,128]{4,3,2,1,0:T(2,128)}, u32[]{:S(2)}) copy-start(f32[1,2,18,2,128]{4,3,2,1,0:T(2,128)} %copy.32) | copy-start | bytes 110596
  108.9 1.3 %copy-start.7 = (f32[32,2,18,256]{3,1,2,0:T(2,128)S(1)}, f32[32,2,18,256]{3,1,2,0:T(2,128)}, u32[]{:S(2)}) copy-start(f32[32,2,18,256]{3,1,2,0:T(2,128)} %reshape.339) | copy-start | bytes 3538948
  108.9 1.6 %copy-start.8 = (bf16[2,256,2,514]{1,0,3,2:T(2,128)(2,1)S(1)}, bf16[2,256,2,514]{1,0,3,2:T(2,128)(2,1)}, u32[]{:S(2)}) copy-start(bf16[2,256,2,514]{1,0,3,2:T(2,128)(2,1)} %convert_element_type.47) | copy-start | bytes 3158020
  108.9 1.6 %copy-start.10 = (f32[2,2,18,256]{3,0,2,1:T(2,128)S(1)}, f32[2,2,18,256]{3,0,2,1:T(2,128)}, u32[]{:S(2)}) copy-start(f32[2,2,18,256]{3,0,2,1:T(2,128)} %copy.57) | copy-start | bytes 221188

commit v2 on v1

--- a/solution.py
+++ b/solution.py
@@ -1,9 +1,12 @@
+import functools
 import math
 
 import jax
 import jax.numpy as jnp
 import numpy as np
 from jax import lax
+from jax.experimental import pallas as pl
+from jax.experimental.pallas import tpu as pltpu
 from jax.sharding import PartitionSpec as P
 
 KR = 256
@@ -83,7 +86,286 @@
     return jnp.transpose(filtered - background / BG, (2, 0, 1))
 
 
+LANES = 128
+MESH = pl.DeviceIdType.MESH
+
+
+def column_planes(samples):
+    phase = (np.arange(COLS)[:, None] * np.arange(samples)[None, :] % samples) * (2.0 * math.pi / samples)
+    planes = np.stack([np.cos(phase), -np.sin(phase)]) / math.sqrt(samples)
+    return jnp.asarray(planes.astype(np.float32).astype(jnp.bfloat16))
+
+
+def row_planes(high):
+    row = np.concatenate([np.arange(high + LANES - 1), [-1]])
+    used = (row <= high)[None, :]
+    sample = np.arange(KR)[:, None] - KR // 2
+    phase = (row[None, :] * sample % ROWS) * (2.0 * math.pi / ROWS)
+    planes = np.stack([np.cos(phase) * used, np.sin(phase) * used]) / math.sqrt(KR)
+    return jnp.asarray(planes.astype(np.float32).astype(jnp.bfloat16))
+
+
+def frame_weights(width, sources, rows):
+    frames = 2 * sources
+    weights = np.zeros((width, frames, rows), np.float32)
+    target = np.arange(frames)
+
+    def place(at, column, frame):
+        series = np.where(target == frame, 1.0, 0.0) - np.where((target - frame) % frames < BG, 1.0 / BG, 0.0)
+        for near in range(max(column - 1, 0), min(column + 2, width)):
+            weights[near, :, at] = series
+
+    for lane in range(2):
+        for source in range(sources):
+            frame = 2 * source + lane
+            for column in range(width):
+                place((lane * sources + source) * width + column, column, frame)
+            for side in range(2):
+                place(2 * sources * width + (lane * sources + source) * 2 + side, (-1, width)[side], frame)
+    return jnp.asarray(weights.reshape(width * frames, rows).astype(jnp.bfloat16))
+
+
+def send_order(count):
+    order = []
+    for away in range(count // 2, 0, -1):
+        order += [away] if 2 * away == count else [away, count - away]
+    return order
+
+
+def product_of(a, b):
+    return lax.dot_general(a, b, (((1,), (0,)), ((), ())), preferred_element_type=jnp.float32)
+
+
+def product_t(a, b):
+    return lax.dot_general(a, b, (((1,), (1,)), ((), ())), preferred_element_type=jnp.float32)
+
+
+def ahead(value, steps):
+    return jnp.concatenate([value[steps:], value[:steps]], axis=0)
+
+
+def kernel(
+    parts, strips, offsets_ref, spectra_hbm, columns_hbm, rows_hbm, weights_hbm, out_ref,
+    spectra, columns, rows, weights, real, imag, edge, main, halo, held, held_halo, lhs, boxed, level,
+    load_sem, own_sem, send_sem, recv_sem, pass_sem, got_sem,
+):
+    me, strip = lax.axis_index("sub"), lax.axis_index("strip")
+    width = COLS // parts
+    depth = spectra.shape[1]
+    samples = spectra.shape[2] // 2
+    high = out_ref.shape[2]
+    other = 1 - strip
+
+    loads = [
+        pltpu.make_async_copy(source, target, load_sem.at[i])
+        for i, (source, target) in enumerate(
+            [(spectra_hbm, spectra), (columns_hbm, columns), (rows_hbm, rows), (weights_hbm, weights)]
+        )
+    ]
+    for load in loads:
+        load.start()
+    barrier = pltpu.get_barrier_semaphore()
+    for away in range(1, parts):
+        pl.semaphore_signal(barrier, inc=1, device_id=(lax.rem(me + away, parts), strip), device_id_type=MESH)
+    pl.semaphore_signal(barrier, inc=1, device_id=(me, other), device_id_type=MESH)
+
+    lane = lax.broadcasted_iota(jnp.int32, (1, 2 * depth), 1)
+    sample = strip * depth + jnp.where(lane < depth, lane, lane - depth) - KR // 2
+    offset = jnp.where(lane < depth, offsets_ref[0], offsets_ref[1])
+    angle = jnp.bitwise_and(offset * sample, ROWS - 1).astype(jnp.float32) * (2.0 * math.pi / ROWS)
+    cosine, sine = jnp.cos(angle), jnp.sin(angle)
+    edge[...] = jnp.zeros_like(edge)
+    loads[0].wait()
+    loads[1].wait()
+    data = spectra[...].reshape(2 * depth, 2 * samples)
+    data_re, data_im = data[:, :samples], data[:, samples:]
+    step = 64
+    for at in range(0, COLS, step):
+        cos_part, sin_part = columns[0, at : at + step], columns[1, at : at + step]
+        re = product_t(cos_part, data_re) - product_t(sin_part, data_im)
+        im = product_t(sin_part, data_re) + product_t(cos_part, data_im)
+        first = at // width
+        for part, value, ref in ((0, re * cosine - im * sine, real), (1, re * sine + im * cosine, imag)):
+            ref[at : at + step] = value
+            blocks = value.reshape(step // width, width, 2 * depth).astype(jnp.bfloat16)
+            for own in range(2):
+                main[first : first + step // width, own * width : (own + 1) * width, part * depth : (part + 1) * depth] = (
+                    blocks[:, :, own * depth : (own + 1) * depth]
+                )
+    for part, ref in ((0, real), (1, imag)):
+        for own in range(2):
+            lanes, into = slice(own * depth, (own + 1) * depth), slice(part * depth, (part + 1) * depth)
+            for d in range(parts):
+                if d > 0:
+                    edge[d, 2 * own : 2 * own + 1, into] = ref[d * width - 1 : d * width, lanes]
+                if d < parts - 1:
+                    edge[d, 2 * own + 1 : 2 * own + 2, into] = ref[(d + 1) * width : (d + 1) * width + 1, lanes]
+    halo[...] = edge[...].astype(jnp.bfloat16)
+
+    pl.semaphore_wait(barrier, parts)
+
+    def sends(to, where):
+        return [
+            pltpu.make_async_remote_copy(
+                src_ref=source.at[to], dst_ref=target.at[strip, where], send_sem=send_sem.at[kind, to],
+                recv_sem=recv_sem.at[kind, where], device_id=(to, strip), device_id_type=MESH,
+            )
+            for kind, source, target in ((0, main, held), (1, halo, held_halo))
+        ]
+
+    def passes(h, source, own=False):
+        return [
+            pltpu.make_async_remote_copy(
+                src_ref=block.at[source] if own else target.at[h, source], dst_ref=target.at[h, source],
+                send_sem=pass_sem.at[kind, source], recv_sem=got_sem.at[kind, source],
+                device_id=(me, other), device_id_type=MESH,
+            )
+            for kind, block, target in ((0, main, held), (1, halo, held_halo))
+        ]
+
+    order = send_order(parts)
+    for away in order:
+        for copy in sends(lax.rem(me + away, parts), me):
+            copy.start()
+    kept = [
+        pltpu.make_async_copy(source.at[me], target.at[strip, me], own_sem.at[kind])
+        for kind, source, target in ((0, main, held), (1, halo, held_halo))
+    ]
+    for copy in passes(strip, me, own=True) + kept:
+        copy.start()
+    for away in reversed(order):
+        source = lax.rem(me + parts - away, parts)
+        for copy in sends(source, source):
+            copy.wait_recv()
+        for copy in passes(strip, source):
+            copy.start()
+    for copy in kept:
+        copy.wait()
+    for away in [0] + order[::-1]:
+        for copy in passes(other, lax.rem(me + parts - away, parts)):
+            copy.wait_recv()
+    for away in order:
+        for copy in sends(lax.rem(me + away, parts), me):
+            copy.wait_send()
+    for away in [0] + order:
+        for copy in passes(strip, lax.rem(me + away, parts), own=away == 0):
+            copy.wait_send()
+
+    top = 2 * parts * width
+    odd = lax.rem(lax.broadcasted_iota(jnp.int32, (1, 1, 2 * depth), 2), 2)
+    sign = 1.0 - 2.0 * (odd * strip).astype(jnp.float32)
+    row_at = lax.broadcasted_iota(jnp.int32, (parts, 8, 2 * depth), 1)
+    for h in range(2):
+        block = held[h].astype(jnp.float32) * sign
+        first, second = block[:, :width], block[:, width:]
+        near = held_halo[h].astype(jnp.float32) * sign
+        near_second = jnp.concatenate([pltpu.roll(near[i], 6, 0)[None] for i in range(parts)], axis=0)
+        for is_halo, one, two in ((False, first, second), (True, near, near_second)):
+            pair = one + two
+            double = pair + ahead(pair, 1)
+            quad = double + ahead(double, 2)
+            for own, frame in ((0, quad), (1, quad - one + ahead(one, WIN // 2))):
+                if is_halo:
+                    frame = jnp.where(row_at < 2, frame, 0.0)
+                    packed = []
+                    for group in range(parts // 4):
+                        total = frame[4 * group]
+                        for j in range(1, 4):
+                            total = total + pltpu.roll(frame[4 * group + j], 2 * j, 0)
+                        packed.append(total)
+                    flat = jnp.concatenate(packed, axis=0).astype(jnp.bfloat16)
+                    at, size = top + own * 2 * parts, 2 * parts
+                else:
+                    flat = frame.reshape(parts * width, 2 * depth).astype(jnp.bfloat16)
+                    at, size = own * parts * width, parts * width
+                for part in range(2):
+                    lhs[at : at + size, part * KR + h * depth : part * KR + (h + 1) * depth] = flat[
+                        :, part * depth : (part + 1) * depth
+                    ]
+
+    loads[2].wait()
+    total_rows = top + 4 * parts
+    tail = lax.broadcasted_iota(jnp.int32, (1, high + LANES), 1)
+    outside = ((tail == high) & (strip == strips - 1)) | ((tail == high + LANES - 1) & (strip == 0))
+    inside = jnp.where(outside, 0.0, 1.0)
+    chunk = 64
+    for at in range(0, total_rows, chunk):
+        left_re, left_im = lhs[at : at + chunk, :KR], lhs[at : at + chunk, KR:]
+        re = product_of(left_re, rows[0]) - product_of(left_im, rows[1])
+        im = product_of(left_re, rows[1]) + product_of(left_im, rows[0])
+        power = jnp.log(1.0 + re * re + im * im) * inside
+        summed = power + pltpu.roll(power, 1, 1) + pltpu.roll(power, high + LANES - 1, 1)
+        boxed[at : at + chunk] = summed[:, :high]
+
+    frames = 2 * parts
+    block = boxed[:top].reshape(frames, width, high)
+    mean = jnp.sum(block, axis=0, keepdims=True) * (1.0 / frames)
+    level[:top] = (block - mean).reshape(top, high).astype(jnp.bfloat16)
+    near = boxed[top:total_rows].reshape(frames // 4, 8, high)
+    mean = jnp.sum(near, axis=0) * (1.0 / frames)
+    mean = mean + pltpu.roll(mean, 4, 0)
+    mean = mean + pltpu.roll(mean, 2, 0)
+    level[top:total_rows] = (near - mean[None]).reshape(total_rows - top, high).astype(jnp.bfloat16)
+    level[total_rows:] = jnp.zeros((level.shape[0] - total_rows, high), jnp.bfloat16)
+    loads[3].wait()
+    for c in range(0, width, 4):
+        piece = product_of(weights[c * frames : (c + 4) * frames], level[...])
+        out_ref[c : c + 4] = (piece * (1.0 / 9.0)).reshape(4, frames, high)
+
+
+def kernel_body(spectra, offsets):
+    parts, strips = lax.axis_size("sub"), lax.axis_size("strip")
+    own, depth, both = spectra.shape
+    width, high = COLS // parts, ROWS // strips
+    frames = own * parts
+    total_rows = frames * (width + 2)
+    padded = -(-total_rows // LANES) * LANES
+    bf16, f32 = jnp.bfloat16, jnp.float32
+    operands = (offsets, spectra, column_planes(both // 2), row_planes(high), frame_weights(width, parts, padded))
+    out = pl.pallas_call(
+        functools.partial(kernel, parts, strips),
+        out_shape=jax.ShapeDtypeStruct((width, frames, high), f32),
+        in_specs=[pl.BlockSpec(memory_space=pltpu.SMEM)] + [pl.BlockSpec(memory_space=pl.ANY)] * 4,
+        out_specs=pl.BlockSpec(memory_space=pltpu.VMEM),
+        scratch_shapes=[pltpu.VMEM(operand.shape, operand.dtype) for operand in operands[1:]]
+        + [
+            pltpu.VMEM((COLS, 2 * depth), f32),
+            pltpu.VMEM((COLS, 2 * depth), f32),
+            pltpu.VMEM((parts, 8, 2 * depth), f32),
+            pltpu.VMEM((parts, 2 * width, 2 * depth), bf16),
+            pltpu.VMEM((parts, 8, 2 * depth), bf16),
+            pltpu.VMEM((strips, parts, 2 * width, 2 * depth), bf16),
+            pltpu.VMEM((strips, parts, 8, 2 * depth), bf16),
+            pltpu.VMEM((total_rows, 2 * KR), bf16),
+            pltpu.VMEM((total_rows, high), f32),
+            pltpu.VMEM((padded, high), bf16),
+            pltpu.SemaphoreType.DMA((4,)),
+            pltpu.SemaphoreType.DMA((2,)),
+            pltpu.SemaphoreType.DMA((2, parts)),
+            pltpu.SemaphoreType.DMA((2, parts)),
+            pltpu.SemaphoreType.DMA((2, parts)),
+            pltpu.SemaphoreType.DMA((2, parts)),
+        ],
+        compiler_params=pltpu.CompilerParams(collective_id=0, has_side_effects=True, vmem_limit_bytes=48 << 20),
+        name="sar",
+    )(*operands)
+    return jnp.transpose(out, (2, 0, 1))
+
+
+def fits(mesh):
+    parts, strips = mesh.shape["sub"], mesh.shape["strip"]
+    return strips == 2 and KR // strips == LANES and COLS % parts == 0 and COLS // parts == 16 and parts % 4 == 0
+
+
+def body(mesh, spectra, offsets):
+    if fits(mesh) and spectra.shape[0] == 2:
+        return kernel_body(spectra, offsets)
+    return plain_body(spectra, offsets)
+
+
 def solution(mesh):
     in_specs = (P("sub", "strip", None), P("sub"))
     out_specs = P("strip", "sub", None)
-    return jax.shard_map(plain_body, mesh=mesh, in_specs=in_specs, out_specs=out_specs, check_vma=False)
+    return jax.shard_map(
+        functools.partial(body, mesh), mesh=mesh, in_specs=in_specs, out_specs=out_specs, check_vma=False
+    )

time: 123 us -> 34.1 us (0.28)
  local copies, waits for them, and re-layouts: 85.5 us -> 6.25 us
  Pallas kernels: 0 us -> 27.5 us
  waiting for transfers between devices: 10.5 us -> 0 us
  other arithmetic: 9.46 us -> 0 us
  starting transfers between devices: 8.96 us -> 0 us
  matrix products: 7.94 us -> 0 us
    slice x64 -> x0, local copies, waits for them, and re-layouts: 52.2 us -> none  [the longest x41 51.1 us: plain_body(): summed = summed + jnp.roll(wider, -lead, axis=0)]
    pallas_call x0 -> x1, Pallas kernels: none -> 27.5 us  [kernel_body(): pl.pallas_call(functools.partial(kernel, parts, strips), out_shape=jax.Sh...]
    dynamic_update_slice x2 -> x0, local copies, waits for them, and re-layouts: 26.1 us -> none  [plain_body(): lax.dynamic_update_slice(whole, part[:, :, :, None], (0, 0, 0, source, 0))]
    all_to_all x1 -> x0, waiting for transfers between devices: 10.5 us -> none  [plain_body(): lax.all_to_all(shifted, 'sub', split_axis=0, concat_axis=0, tiled=True)]
    dot_general x2 -> x0, matrix products: 7.94 us -> none  [the longest x1 5.03 us: plain_body(): jnp.einsum('fpnk,pkqm->qnfm', summed.astype(jnp.bfloat16), row_table(rows...]
    all_to_all x1 -> x0, starting transfers between devices: 7.41 us -> none  [plain_body(): lax.all_to_all(shifted, 'sub', split_axis=0, concat_axis=0, tiled=True)]
    transpose x1 -> x0, other arithmetic: 4.87 us -> none  [plain_body(): return jnp.transpose(filtered - background / BG, (2, 0, 1))]
    unnamed x24 -> x11, local copies, waits for them, and re-layouts: 1.71 us -> 6.25 us
  transfers between devices with their start and end apart: 2 -> 0, of which waited for: 1 -> 0; matrix products, arithmetic and copies ran while one was open for 14% -> 0% of each run, Pallas kernels for 0% -> 0%
where the time goes in v2:
time: 34.1 us; the launch traced here: 33.8 us
  Pallas kernels  27.5 us (81%)
  local copies, waits for them, and re-layouts  6.25 us (18%)
    pallas_call x1, Pallas kernels, kernel_body(): pl.pallas_call(functools.partial(kernel, parts, strips), out_shape=jax.Sh...  27.5 us
    unnamed x11, local copies, waits for them, and re-layouts  6.25 us

profile of v2, /device:TPU:0, one launch (start us, length us, event | category | flops | bytes accessed | tf_op | source)
XLA Modules:
  0.0 33.8 jit_solution(9236062425499767008)
XLA Ops:
  0.0 0.0 copy-start
  0.0 1.2 %copy-done = bf16[2,128,2048]{2,1,0:T(8,128)(2,1)S(1)} copy-done((bf16[2,128,2048]{2,1,0:T(8,128)(2,1)S(1)}, bf16[2,128,2048]{2,1,0:T(8,128)(2,1)}, u32[]{:S(2)}) %copy-start) | copy-done | bytes 1048600
  1.2 0.0 copy-start.1
  1.2 1.2 %copy-done.1 = bf16[2,256,1024]{2,1,0:T(8,128)(2,1)S(1)} copy-done((bf16[2,256,1024]{2,1,0:T(8,128)(2,1)S(1)}, bf16[2,256,1024]{2,1,0:T(8,128)(2,1)}, u32[]{:S(2)}) %copy-start.1) | copy-done | bytes 1048600
  2.5 0.0 copy-start.2
  2.5 1.1 %copy-done.2 = bf16[512,640]{1,0:T(8,128)(2,1)S(1)} copy-done((bf16[512,640]{1,0:T(8,128)(2,1)S(1)}, bf16[512,640]{1,0:T(8,128)(2,1)}, u32[]{:S(2)}) %copy-start.2) | copy-done | bytes 655384
  3.5 0.0 copy-start.3
  3.5 1.1 %copy-done.3 = bf16[2,256,640]{2,1,0:T(8,128)(2,1)S(1)} copy-done((bf16[2,256,640]{2,1,0:T(8,128)(2,1)S(1)}, bf16[2,256,640]{2,1,0:T(8,128)(2,1)}, u32[]{:S(2)}) %copy-start.3) | copy-done | bytes 655384
  4.6 0.0 copy-start.4
  4.6 0.7 %copy-done.4 = s32[2]{0:T(128)S(1)} copy-done((s32[2]{0:T(128)S(1)}, s32[2]{0:T(128)}, u32[]{:S(2)}) %copy-start.4) | copy-done | bytes 32
  5.3 27.5 %sar.1 = f32[16,32,512]{2,1,0:T(8,128)S(1)} custom-call(s32[2]{0:T(128)S(1)} %copy-done.4, bf16[2,128,2048]{2,1,0:T(8,128)(2,1)S(1)} %copy-done, bf16[2,256,1024]{2,1,0:T(8,128)(2,1)S(1)} %copy-done.1, bf16[2,256,640]{2,1,0:T(8,128)(2,1)S(1)} %copy-done.3, bf16[512,640]{1,0:T(8,128)(2,1)S(1)} %copy-done.2), custom_call_target="tpu_custom_call" | custom-call | tf_op jit(solution)/shard_map/sar/pallas_call | solution.py:325
  32.8 1.0 %copy.7 = f32[512,16,32]{0,2,1:T(8,128)} copy(f32[512,16,32]{0,2,1:T(8,128)S(1)} %bitcast.1) | data formatting | bytes 2097152
Async XLA Ops:
  0.0 1.2 %copy-start = (bf16[2,128,2048]{2,1,0:T(8,128)(2,1)S(1)}, bf16[2,128,2048]{2,1,0:T(8,128)(2,1)}, u32[]{:S(2)}) copy-start(bf16[2,128,2048]{2,1,0:T(8,128)(2,1)} %spectra_hbm.1) | copy-start | bytes 3145732
  1.2 1.2 %copy-start.1 = (bf16[2,256,1024]{2,1,0:T(8,128)(2,1)S(1)}, bf16[2,256,1024]{2,1,0:T(8,128)(2,1)}, u32[]{:S(2)}) copy-start(bf16[2,256,1024]{2,1,0:T(8,128)(2,1)} %constant.6.clone.columns_hbm) | copy-start | bytes 3145732
  2.5 1.1 %copy-start.2 = (bf16[512,640]{1,0:T(8,128)(2,1)S(1)}, bf16[512,640]{1,0:T(8,128)(2,1)}, u32[]{:S(2)}) copy-start(bf16[512,640]{1,0:T(8,128)(2,1)} %constant.8.clone.weights_hbm) | copy-start | bytes 1966084
  3.5 1.1 %copy-start.3 = (bf16[2,256,640]{2,1,0:T(8,128)(2,1)S(1)}, bf16[2,256,640]{2,1,0:T(8,128)(2,1)}, u32[]{:S(2)}) copy-start(bf16[2,256,640]{2,1,0:T(8,128)(2,1)} %constant.7.clone.rows_hbm) | copy-start | bytes 1966084
  4.6 0.7 %copy-start.4 = (s32[2]{0:T(128)S(1)}, s32[2]{0:T(128)}, u32[]{:S(2)}) copy-start(s32[2]{0:T(128)} %offsets_ref.1) | copy-start | bytes 28

commit v3 on v2

--- a/solution.py
+++ b/solution.py
@@ -145,8 +145,8 @@
 
 
 def kernel(
-    parts, strips, offsets_ref, spectra_hbm, columns_hbm, rows_hbm, weights_hbm, out_ref,
-    spectra, columns, rows, weights, real, imag, edge, main, halo, held, held_halo, lhs, boxed, level,
+    parts, strips, offsets_hbm, spectra_hbm, columns_hbm, rows_hbm, weights_hbm, out_ref,
+    offsets_ref, spectra, columns, rows, weights, real, imag, edge, main, halo, held, held_halo, lhs, boxed, level,
     load_sem, own_sem, send_sem, recv_sem, pass_sem, got_sem,
 ):
     me, strip = lax.axis_index("sub"), lax.axis_index("strip")
@@ -159,7 +159,7 @@
     loads = [
         pltpu.make_async_copy(source, target, load_sem.at[i])
         for i, (source, target) in enumerate(
-            [(spectra_hbm, spectra), (columns_hbm, columns), (rows_hbm, rows), (weights_hbm, weights)]
+            [(offsets_hbm, offsets_ref), (spectra_hbm, spectra), (columns_hbm, columns), (rows_hbm, rows), (weights_hbm, weights)]
         )
     ]
     for load in loads:
@@ -169,14 +169,15 @@
         pl.semaphore_signal(barrier, inc=1, device_id=(lax.rem(me + away, parts), strip), device_id_type=MESH)
     pl.semaphore_signal(barrier, inc=1, device_id=(me, other), device_id_type=MESH)
 
+    loads[0].wait()
     lane = lax.broadcasted_iota(jnp.int32, (1, 2 * depth), 1)
     sample = strip * depth + jnp.where(lane < depth, lane, lane - depth) - KR // 2
     offset = jnp.where(lane < depth, offsets_ref[0], offsets_ref[1])
     angle = jnp.bitwise_and(offset * sample, ROWS - 1).astype(jnp.float32) * (2.0 * math.pi / ROWS)
     cosine, sine = jnp.cos(angle), jnp.sin(angle)
     edge[...] = jnp.zeros_like(edge)
-    loads[0].wait()
     loads[1].wait()
+    loads[2].wait()
     data = spectra[...].reshape(2 * depth, 2 * samples)
     data_re, data_im = data[:, :samples], data[:, samples:]
     step = 64
@@ -283,7 +284,7 @@
                         :, part * depth : (part + 1) * depth
                     ]
 
-    loads[2].wait()
+    loads[3].wait()
     total_rows = top + 4 * parts
     tail = lax.broadcasted_iota(jnp.int32, (1, high + LANES), 1)
     outside = ((tail == high) & (strip == strips - 1)) | ((tail == high + LANES - 1) & (strip == 0))
@@ -307,7 +308,7 @@
     mean = mean + pltpu.roll(mean, 2, 0)
     level[top:total_rows] = (near - mean[None]).reshape(total_rows - top, high).astype(jnp.bfloat16)
     level[total_rows:] = jnp.zeros((level.shape[0] - total_rows, high), jnp.bfloat16)
-    loads[3].wait()
+    loads[4].wait()
     for c in range(0, width, 4):
         piece = product_of(weights[c * frames : (c + 4) * frames], level[...])
         out_ref[c : c + 4] = (piece * (1.0 / 9.0)).reshape(4, frames, high)
@@ -325,9 +326,10 @@
     out = pl.pallas_call(
         functools.partial(kernel, parts, strips),
         out_shape=jax.ShapeDtypeStruct((width, frames, high), f32),
-        in_specs=[pl.BlockSpec(memory_space=pltpu.SMEM)] + [pl.BlockSpec(memory_space=pl.ANY)] * 4,
+        in_specs=[pl.BlockSpec(memory_space=pltpu.HBM)] * 5,
         out_specs=pl.BlockSpec(memory_space=pltpu.VMEM),
-        scratch_shapes=[pltpu.VMEM(operand.shape, operand.dtype) for operand in operands[1:]]
+        scratch_shapes=[pltpu.SMEM(offsets.shape, offsets.dtype)]
+        + [pltpu.VMEM(operand.shape, operand.dtype) for operand in operands[1:]]
         + [
             pltpu.VMEM((COLS, 2 * depth), f32),
             pltpu.VMEM((COLS, 2 * depth), f32),
@@ -339,7 +341,7 @@
             pltpu.VMEM((total_rows, 2 * KR), bf16),
             pltpu.VMEM((total_rows, high), f32),
             pltpu.VMEM((padded, high), bf16),
-            pltpu.SemaphoreType.DMA((4,)),
+            pltpu.SemaphoreType.DMA((5,)),
             pltpu.SemaphoreType.DMA((2,)),
             pltpu.SemaphoreType.DMA((2, parts)),
             pltpu.SemaphoreType.DMA((2, parts)),
@@ -348,7 +350,7 @@
         ],
         compiler_params=pltpu.CompilerParams(collective_id=0, has_side_effects=True, vmem_limit_bytes=48 << 20),
         name="sar",
-    )(*operands)
+    )(*(pltpu.with_memory_space_constraint(operand, pltpu.HBM) for operand in operands))
     return jnp.transpose(out, (2, 0, 1))
 
 

time: 34.1 us -> 28.9 us (0.85)
  local copies, waits for them, and re-layouts: 6.25 us -> 0.97 us
    unnamed x11 -> x1, local copies, waits for them, and re-layouts: 6.25 us -> 0.97 us
where the time goes in v3:
time: 28.9 us; the launch traced here: 28.7 us
  Pallas kernels  27.8 us (96%)
  local copies, waits for them, and re-layouts  0.97 us (3%)
    pallas_call x1, Pallas kernels, kernel_body(): pl.pallas_call(functools.partial(kernel, parts, strips), out_shape=jax.Sh...  27.8 us
    unnamed x1, local copies, waits for them, and re-layouts  0.97 us

profile of v3, /device:TPU:0, one launch (start us, length us, event | category | flops | bytes accessed | tf_op | source)
XLA Modules:
  0.0 28.7 jit_solution(11434574508578976805)
XLA Ops:
  0.0 27.8 %sar.1 = f32[16,32,512]{2,1,0:T(8,128)S(1)} custom-call(s32[2]{0:T(128)} %offsets_hbm.1, bf16[2,128,2048]{2,1,0:T(8,128)(2,1)} %spectra_hbm.1, bf16[2,256,1024]{2,1,0:T(8,128)(2,1)} %constant.6.clone.columns_hbm, bf16[2,256,640]{2,1,0:T(8,128)(2,1)} %constant.7.clone.rows_hbm, bf16[512,640]{1,0:T(8,128)(2,1)} %constant.8.clone.weights_hbm), custom_call_target="tpu_custom_call" | custom-call | tf_op jit(solution)/shard_map/sar/pallas_call | solution.py:326
  27.8 1.0 %copy.7 = f32[512,16,32]{0,2,1:T(8,128)} copy(f32[512,16,32]{0,2,1:T(8,128)S(1)} %bitcast.1) | data formatting | bytes 2097152

commit v4 on v3

--- a/solution.py
+++ b/solution.py
@@ -162,7 +162,7 @@
             [(offsets_hbm, offsets_ref), (spectra_hbm, spectra), (columns_hbm, columns), (rows_hbm, rows), (weights_hbm, weights)]
         )
     ]
-    for load in loads:
+    for load in loads[:3]:
         load.start()
     barrier = pltpu.get_barrier_semaphore()
     for away in range(1, parts):
@@ -178,9 +178,11 @@
     edge[...] = jnp.zeros_like(edge)
     loads[1].wait()
     loads[2].wait()
+    for load in loads[3:]:
+        load.start()
     data = spectra[...].reshape(2 * depth, 2 * samples)
     data_re, data_im = data[:, :samples], data[:, samples:]
-    step = 64
+    step = COLS
     for at in range(0, COLS, step):
         cos_part, sin_part = columns[0, at : at + step], columns[1, at : at + step]
         re = product_t(cos_part, data_re) - product_t(sin_part, data_im)
@@ -240,23 +242,11 @@
             copy.wait_recv()
         for copy in passes(strip, source):
             copy.start()
-    for copy in kept:
-        copy.wait()
-    for away in [0] + order[::-1]:
-        for copy in passes(other, lax.rem(me + parts - away, parts)):
-            copy.wait_recv()
-    for away in order:
-        for copy in sends(lax.rem(me + away, parts), me):
-            copy.wait_send()
-    for away in [0] + order:
-        for copy in passes(strip, lax.rem(me + away, parts), own=away == 0):
-            copy.wait_send()
-
     top = 2 * parts * width
     odd = lax.rem(lax.broadcasted_iota(jnp.int32, (1, 1, 2 * depth), 2), 2)
     sign = 1.0 - 2.0 * (odd * strip).astype(jnp.float32)
     row_at = lax.broadcasted_iota(jnp.int32, (parts, 8, 2 * depth), 1)
-    for h in range(2):
+    def window(h):
         block = held[h].astype(jnp.float32) * sign
         first, second = block[:, :width], block[:, width:]
         near = held_halo[h].astype(jnp.float32) * sign
@@ -280,16 +270,23 @@
                     flat = frame.reshape(parts * width, 2 * depth).astype(jnp.bfloat16)
                     at, size = own * parts * width, parts * width
                 for part in range(2):
-                    lhs[at : at + size, part * KR + h * depth : part * KR + (h + 1) * depth] = flat[
+                    lhs[at : at + size, pl.ds(pl.multiple_of(part * KR + h * depth, depth), depth)] = flat[
                         :, part * depth : (part + 1) * depth
                     ]
 
+    for copy in kept:
+        copy.wait()
+    window(strip)
+    for away in [0] + order[::-1]:
+        for copy in passes(other, lax.rem(me + parts - away, parts)):
+            copy.wait_recv()
+    window(other)
     loads[3].wait()
     total_rows = top + 4 * parts
     tail = lax.broadcasted_iota(jnp.int32, (1, high + LANES), 1)
     outside = ((tail == high) & (strip == strips - 1)) | ((tail == high + LANES - 1) & (strip == 0))
     inside = jnp.where(outside, 0.0, 1.0)
-    chunk = 64
+    chunk = total_rows // 3
     for at in range(0, total_rows, chunk):
         left_re, left_im = lhs[at : at + chunk, :KR], lhs[at : at + chunk, KR:]
         re = product_of(left_re, rows[0]) - product_of(left_im, rows[1])
@@ -312,6 +309,12 @@
     for c in range(0, width, 4):
         piece = product_of(weights[c * frames : (c + 4) * frames], level[...])
         out_ref[c : c + 4] = (piece * (1.0 / 9.0)).reshape(4, frames, high)
+    for away in order:
+        for copy in sends(lax.rem(me + away, parts), me):
+            copy.wait_send()
+    for away in [0] + order:
+        for copy in passes(strip, lax.rem(me + away, parts), own=away == 0):
+            copy.wait_send()
 
 
 def kernel_body(spectra, offsets):

time: 28.9 us -> 26.4 us (0.913)
  Pallas kernels: 27.8 us -> 25.3 us
    pallas_call x1, Pallas kernels: 27.8 us -> 25.3 us  [kernel_body(): pl.pallas_call(functools.partial(kernel, parts, strips), out_shape=jax.Sh...]
where the time goes in v4:
time: 26.4 us; the launch traced here: 26.2 us
  Pallas kernels  25.3 us (96%)
  local copies, waits for them, and re-layouts  0.97 us (4%)
    pallas_call x1, Pallas kernels, kernel_body(): pl.pallas_call(functools.partial(kernel, parts, strips), out_shape=jax.Sh...  25.3 us
    unnamed x1, local copies, waits for them, and re-layouts  0.97 us

profile of v4, /device:TPU:0, one launch (start us, length us, event | category | flops | bytes accessed | tf_op | source)
XLA Modules:
  0.0 26.2 jit_solution(18131403250864661323)
XLA Ops:
  0.0 25.3 %sar.1 = f32[16,32,512]{2,1,0:T(8,128)S(1)} custom-call(s32[2]{0:T(128)} %offsets_hbm.1, bf16[2,128,2048]{2,1,0:T(8,128)(2,1)} %spectra_hbm.1, bf16[2,256,1024]{2,1,0:T(8,128)(2,1)} %constant.6.clone.columns_hbm, bf16[2,256,640]{2,1,0:T(8,128)(2,1)} %constant.7.clone.rows_hbm, bf16[512,640]{1,0:T(8,128)(2,1)} %constant.8.clone.weights_hbm), custom_call_target="tpu_custom_call" | custom-call | tf_op jit(solution)/shard_map/sar/pallas_call | solution.py:329
  25.3 1.0 %copy.7 = f32[512,16,32]{0,2,1:T(8,128)} copy(f32[512,16,32]{0,2,1:T(8,128)S(1)} %bitcast.1) | data formatting | bytes 2097152

commit v5 on v4

--- a/solution.py
+++ b/solution.py
@@ -87,6 +87,7 @@
 
 
 LANES = 128
+GROUP = 4
 MESH = pl.DeviceIdType.MESH
 
 
@@ -125,11 +126,11 @@
     return jnp.asarray(weights.reshape(width * frames, rows).astype(jnp.bfloat16))
 
 
-def send_order(count):
-    order = []
-    for away in range(count // 2, 0, -1):
-        order += [away] if 2 * away == count else [away, count - away]
-    return order
+def send_order(layers, group):
+    order = [(0, place) for place in range(1, group)]
+    half = layers // 2
+    turn = [half] + [layer for away in range(half - 1, 0, -1) for layer in (half - away, half + away)]
+    return order + [(layer, place) for place in range(group) for layer in turn]
 
 
 def product_of(a, b):
@@ -203,7 +204,7 @@
                     edge[d, 2 * own : 2 * own + 1, into] = ref[d * width - 1 : d * width, lanes]
                 if d < parts - 1:
                     edge[d, 2 * own + 1 : 2 * own + 2, into] = ref[(d + 1) * width : (d + 1) * width + 1, lanes]
-    halo[...] = edge[...].astype(jnp.bfloat16)
+    halo[...] = edge[:, :4].astype(jnp.bfloat16)
 
     pl.semaphore_wait(barrier, parts)
 
@@ -226,9 +227,17 @@
             for kind, block, target in ((0, main, held), (1, halo, held_halo))
         ]
 
-    order = send_order(parts)
+    layers = parts // GROUP
+    order = send_order(layers, GROUP)
+
+    def device_at(layer, place):
+        return lax.rem(me // GROUP + layer, layers) * GROUP + lax.rem(lax.rem(me, GROUP) + place, GROUP)
+
+    def device_from(layer, place):
+        return device_at(layers - layer, GROUP - place)
+
     for away in order:
-        for copy in sends(lax.rem(me + away, parts), me):
+        for copy in sends(device_at(*away), me):
             copy.start()
     kept = [
         pltpu.make_async_copy(source.at[me], target.at[strip, me], own_sem.at[kind])
@@ -236,8 +245,8 @@
     ]
     for copy in passes(strip, me, own=True) + kept:
         copy.start()
-    for away in reversed(order):
-        source = lax.rem(me + parts - away, parts)
+    for away in order:
+        source = device_from(*away)
         for copy in sends(source, source):
             copy.wait_recv()
         for copy in passes(strip, source):
@@ -250,6 +259,7 @@
         block = held[h].astype(jnp.float32) * sign
         first, second = block[:, :width], block[:, width:]
         near = held_halo[h].astype(jnp.float32) * sign
+        near = jnp.concatenate([near, jnp.zeros_like(near)], axis=1)
         near_second = jnp.concatenate([pltpu.roll(near[i], 6, 0)[None] for i in range(parts)], axis=0)
         for is_halo, one, two in ((False, first, second), (True, near, near_second)):
             pair = one + two
@@ -277,8 +287,8 @@
     for copy in kept:
         copy.wait()
     window(strip)
-    for away in [0] + order[::-1]:
-        for copy in passes(other, lax.rem(me + parts - away, parts)):
+    for away in [(0, 0)] + order:
+        for copy in passes(other, device_from(*away)):
             copy.wait_recv()
     window(other)
     loads[3].wait()
@@ -310,10 +320,10 @@
         piece = product_of(weights[c * frames : (c + 4) * frames], level[...])
         out_ref[c : c + 4] = (piece * (1.0 / 9.0)).reshape(4, frames, high)
     for away in order:
-        for copy in sends(lax.rem(me + away, parts), me):
+        for copy in sends(device_at(*away), me):
             copy.wait_send()
-    for away in [0] + order:
-        for copy in passes(strip, lax.rem(me + away, parts), own=away == 0):
+    for away in [(0, 0)] + order:
+        for copy in passes(strip, device_from(*away), own=away == (0, 0)):
             copy.wait_send()
 
 
@@ -338,9 +348,9 @@
             pltpu.VMEM((COLS, 2 * depth), f32),
             pltpu.VMEM((parts, 8, 2 * depth), f32),
             pltpu.VMEM((parts, 2 * width, 2 * depth), bf16),
-            pltpu.VMEM((parts, 8, 2 * depth), bf16),
+            pltpu.VMEM((parts, 4, 2 * depth), bf16),
             pltpu.VMEM((strips, parts, 2 * width, 2 * depth), bf16),
-            pltpu.VMEM((strips, parts, 8, 2 * depth), bf16),
+            pltpu.VMEM((strips, parts, 4, 2 * depth), bf16),
             pltpu.VMEM((total_rows, 2 * KR), bf16),
             pltpu.VMEM((total_rows, high), f32),
             pltpu.VMEM((padded, high), bf16),

time: 26.4 us -> 23.2 us (0.88)
  Pallas kernels: 25.3 us -> 22.1 us
    pallas_call x1, Pallas kernels: 25.3 us -> 22.1 us  [kernel_body(): pl.pallas_call(functools.partial(kernel, parts, strips), out_shape=jax.Sh...]
where the time goes in v5:
time: 23.2 us; the launch traced here: 23.1 us
  Pallas kernels  22.1 us (95%)
  local copies, waits for them, and re-layouts  0.97 us (4%)
    pallas_call x1, Pallas kernels, kernel_body(): pl.pallas_call(functools.partial(kernel, parts, strips), out_shape=jax.Sh...  22.1 us
    unnamed x1, local copies, waits for them, and re-layouts  0.97 us

profile of v5, /device:TPU:0, one launch (start us, length us, event | category | flops | bytes accessed | tf_op | source)
XLA Modules:
  0.0 23.1 jit_solution(9953571146195630040)
XLA Ops:
  0.0 22.1 %sar.1 = f32[16,32,512]{2,1,0:T(8,128)S(1)} custom-call(s32[2]{0:T(128)} %offsets_hbm.1, bf16[2,128,2048]{2,1,0:T(8,128)(2,1)} %spectra_hbm.1, bf16[2,256,1024]{2,1,0:T(8,128)(2,1)} %constant.6.clone.columns_hbm, bf16[2,256,640]{2,1,0:T(8,128)(2,1)} %constant.7.clone.rows_hbm, bf16[512,640]{1,0:T(8,128)(2,1)} %constant.8.clone.weights_hbm), custom_call_target="tpu_custom_call" | custom-call | tf_op jit(solution)/shard_map/sar/pallas_call | solution.py:339
  22.1 1.0 %copy.7 = f32[512,16,32]{0,2,1:T(8,128)} copy(f32[512,16,32]{0,2,1:T(8,128)S(1)} %bitcast.1) | data formatting | bytes 2097152

commit v6 on v5

--- a/solution.py
+++ b/solution.py
@@ -130,7 +130,7 @@
     order = [(0, place) for place in range(1, group)]
     half = layers // 2
     turn = [half] + [layer for away in range(half - 1, 0, -1) for layer in (half - away, half + away)]
-    return order + [(layer, place) for place in range(group) for layer in turn]
+    return order + [(layer, place) for place in range(group) for layer in turn[1:]] + [(half, place) for place in range(group)]
 
 
 def product_of(a, b):

time: 23.2 us -> 22.7 us (0.978)
  Pallas kernels: 22.1 us -> 21.6 us
    pallas_call x1, Pallas kernels: 22.1 us -> 21.6 us  [kernel_body(): pl.pallas_call(functools.partial(kernel, parts, strips), out_shape=jax.Sh...]
where the time goes in v6:
time: 22.7 us; the launch traced here: 22.6 us
  Pallas kernels  21.6 us (95%)
  local copies, waits for them, and re-layouts  0.97 us (4%)
    pallas_call x1, Pallas kernels, kernel_body(): pl.pallas_call(functools.partial(kernel, parts, strips), out_shape=jax.Sh...  21.6 us
    unnamed x1, local copies, waits for them, and re-layouts  0.97 us

profile of v6, /device:TPU:0, one launch (start us, length us, event | category | flops | bytes accessed | tf_op | source)
XLA Modules:
  0.0 22.6 jit_solution(3220935030843799457)
XLA Ops:
  0.0 21.6 %sar.1 = f32[16,32,512]{2,1,0:T(8,128)S(1)} custom-call(s32[2]{0:T(128)} %offsets_hbm.1, bf16[2,128,2048]{2,1,0:T(8,128)(2,1)} %spectra_hbm.1, bf16[2,256,1024]{2,1,0:T(8,128)(2,1)} %constant.6.clone.columns_hbm, bf16[2,256,640]{2,1,0:T(8,128)(2,1)} %constant.7.clone.rows_hbm, bf16[512,640]{1,0:T(8,128)(2,1)} %constant.8.clone.weights_hbm), custom_call_target="tpu_custom_call" | custom-call | tf_op jit(solution)/shard_map/sar/pallas_call | solution.py:339
  21.6 1.0 %copy.7 = f32[512,16,32]{0,2,1:T(8,128)} copy(f32[512,16,32]{0,2,1:T(8,128)S(1)} %bitcast.1) | data formatting | bytes 2097152

commit v7 on v6

--- a/solution.py
+++ b/solution.py
@@ -147,7 +147,7 @@
 
 def kernel(
     parts, strips, offsets_hbm, spectra_hbm, columns_hbm, rows_hbm, weights_hbm, out_ref,
-    offsets_ref, spectra, columns, rows, weights, real, imag, edge, main, halo, held, held_halo, lhs, boxed, level,
+    offsets_ref, spectra, columns, rows, weights, real, imag, edge, main, held, lhs, boxed, level,
     load_sem, own_sem, send_sem, recv_sem, pass_sem, got_sem,
 ):
     me, strip = lax.axis_index("sub"), lax.axis_index("strip")
@@ -191,11 +191,11 @@
         first = at // width
         for part, value, ref in ((0, re * cosine - im * sine, real), (1, re * sine + im * cosine, imag)):
             ref[at : at + step] = value
-            blocks = value.reshape(step // width, width, 2 * depth).astype(jnp.bfloat16)
+            blocks = value.reshape(step // width, width // 4, 4, 2 * depth).astype(jnp.bfloat16)
             for own in range(2):
-                main[first : first + step // width, own * width : (own + 1) * width, part * depth : (part + 1) * depth] = (
-                    blocks[:, :, own * depth : (own + 1) * depth]
-                )
+                main[
+                    first : first + step // width, own * width // 4 : (own + 1) * width // 4, :, part * depth : (part + 1) * depth
+                ] = blocks[:, :, :, own * depth : (own + 1) * depth]
     for part, ref in ((0, real), (1, imag)):
         for own in range(2):
             lanes, into = slice(own * depth, (own + 1) * depth), slice(part * depth, (part + 1) * depth)
@@ -204,7 +204,7 @@
                     edge[d, 2 * own : 2 * own + 1, into] = ref[d * width - 1 : d * width, lanes]
                 if d < parts - 1:
                     edge[d, 2 * own + 1 : 2 * own + 2, into] = ref[(d + 1) * width : (d + 1) * width + 1, lanes]
-    halo[...] = edge[:, :4].astype(jnp.bfloat16)
+    main[:, 2 * width // 4] = edge[:, :4].astype(jnp.bfloat16)
 
     pl.semaphore_wait(barrier, parts)
 
@@ -214,7 +214,7 @@
                 src_ref=source.at[to], dst_ref=target.at[strip, where], send_sem=send_sem.at[kind, to],
                 recv_sem=recv_sem.at[kind, where], device_id=(to, strip), device_id_type=MESH,
             )
-            for kind, source, target in ((0, main, held), (1, halo, held_halo))
+            for kind, source, target in ((0, main, held),)
         ]
 
     def passes(h, source, own=False):
@@ -224,7 +224,7 @@
                 send_sem=pass_sem.at[kind, source], recv_sem=got_sem.at[kind, source],
                 device_id=(me, other), device_id_type=MESH,
             )
-            for kind, block, target in ((0, main, held), (1, halo, held_halo))
+            for kind, block, target in ((0, main, held),)
         ]
 
     layers = parts // GROUP
@@ -241,7 +241,7 @@
             copy.start()
     kept = [
         pltpu.make_async_copy(source.at[me], target.at[strip, me], own_sem.at[kind])
-        for kind, source, target in ((0, main, held), (1, halo, held_halo))
+        for kind, source, target in ((0, main, held),)
     ]
     for copy in passes(strip, me, own=True) + kept:
         copy.start()
@@ -256,9 +256,10 @@
     sign = 1.0 - 2.0 * (odd * strip).astype(jnp.float32)
     row_at = lax.broadcasted_iota(jnp.int32, (parts, 8, 2 * depth), 1)
     def window(h):
-        block = held[h].astype(jnp.float32) * sign
+        whole = held[h].astype(jnp.float32) * sign[None]
+        block = whole[:, : 2 * width // 4].reshape(parts, 2 * width, 2 * depth)
         first, second = block[:, :width], block[:, width:]
-        near = held_halo[h].astype(jnp.float32) * sign
+        near = whole[:, 2 * width // 4]
         near = jnp.concatenate([near, jnp.zeros_like(near)], axis=1)
         near_second = jnp.concatenate([pltpu.roll(near[i], 6, 0)[None] for i in range(parts)], axis=0)
         for is_halo, one, two in ((False, first, second), (True, near, near_second)):
@@ -347,19 +348,17 @@
             pltpu.VMEM((COLS, 2 * depth), f32),
             pltpu.VMEM((COLS, 2 * depth), f32),
             pltpu.VMEM((parts, 8, 2 * depth), f32),
-            pltpu.VMEM((parts, 2 * width, 2 * depth), bf16),
-            pltpu.VMEM((parts, 4, 2 * depth), bf16),
-            pltpu.VMEM((strips, parts, 2 * width, 2 * depth), bf16),
-            pltpu.VMEM((strips, parts, 4, 2 * depth), bf16),
+            pltpu.VMEM((parts, 2 * width // 4 + 1, 4, 2 * depth), bf16),
+            pltpu.VMEM((strips, parts, 2 * width // 4 + 1, 4, 2 * depth), bf16),
             pltpu.VMEM((total_rows, 2 * KR), bf16),
             pltpu.VMEM((total_rows, high), f32),
             pltpu.VMEM((padded, high), bf16),
             pltpu.SemaphoreType.DMA((5,)),
-            pltpu.SemaphoreType.DMA((2,)),
-            pltpu.SemaphoreType.DMA((2, parts)),
-            pltpu.SemaphoreType.DMA((2, parts)),
-            pltpu.SemaphoreType.DMA((2, parts)),
-            pltpu.SemaphoreType.DMA((2, parts)),
+            pltpu.SemaphoreType.DMA((1,)),
+            pltpu.SemaphoreType.DMA((1, parts)),
+            pltpu.SemaphoreType.DMA((1, parts)),
+            pltpu.SemaphoreType.DMA((1, parts)),
+            pltpu.SemaphoreType.DMA((1, parts)),
         ],
         compiler_params=pltpu.CompilerParams(collective_id=0, has_side_effects=True, vmem_limit_bytes=48 << 20),
         name="sar",

time: 22.7 us -> 22.2 us (0.978)
  Pallas kernels: 21.6 us -> 21 us
    pallas_call x1, Pallas kernels: 21.6 us -> 21 us  [kernel_body(): pl.pallas_call(functools.partial(kernel, parts, strips), out_shape=jax.Sh...]
where the time goes in v7:
time: 22.2 us; the launch traced here: 22 us
  Pallas kernels  21 us (95%)
  local copies, waits for them, and re-layouts  0.97 us (4%)
    pallas_call x1, Pallas kernels, kernel_body(): pl.pallas_call(functools.partial(kernel, parts, strips), out_shape=jax.Sh...  21 us
    unnamed x1, local copies, waits for them, and re-layouts  0.97 us

profile of v7, /device:TPU:0, one launch (start us, length us, event | category | flops | bytes accessed | tf_op | source)
XLA Modules:
  0.0 22.0 jit_solution(2814662575265935832)
XLA Ops:
  0.0 21.0 %sar.1 = f32[16,32,512]{2,1,0:T(8,128)S(1)} custom-call(s32[2]{0:T(128)} %offsets_hbm.1, bf16[2,128,2048]{2,1,0:T(8,128)(2,1)} %spectra_hbm.1, bf16[2,256,1024]{2,1,0:T(8,128)(2,1)} %constant.6.clone.columns_hbm, bf16[2,256,640]{2,1,0:T(8,128)(2,1)} %constant.7.clone.rows_hbm, bf16[512,640]{1,0:T(8,128)(2,1)} %constant.8.clone.weights_hbm), custom_call_target="tpu_custom_call" | custom-call | tf_op jit(solution)/shard_map/sar/pallas_call | solution.py:340
  21.0 1.0 %copy.7 = f32[512,16,32]{0,2,1:T(8,128)} copy(f32[512,16,32]{0,2,1:T(8,128)S(1)} %bitcast.1) | data formatting | bytes 2097152
